TPU v7x, 256 devices: a whole 4x4x8 slice. The times are simulated.
256 devices in a mesh: gx: 8 (over y, core), gy: 32 (over x, z).
Axes of the slice: x: 4, y: 4, z: 8, core: 2. Of those that a mesh axis runs over, the one named last changes fastest.
Arguments:
- hidden_in: bfloat16 [8192, 2560], P(('gx', 'gy')), may hold values from -6 to 6
- norm_gain: float32 [2560], replicated, may hold values from 0.1 to 1.9
- router_weight: bfloat16 [2560, 64], replicated, may hold values from -0.0625 to 0.0625
- expert_ids: int32 [8192, 6], P(('gx', 'gy')), may hold values from 0 to 63, all different within a row; in each aligned block of 32 rows (0 to 31, 32 to 63, ...) at most 4 rows name the same one
- expert_gate: bfloat16 [64, 2560, 1536], P('gy', None, 'gx'), may hold values from -0.125 to 0.125
- expert_up: bfloat16 [64, 2560, 1536], P('gy', None, 'gx'), may hold values from -0.125 to 0.125
- expert_down: bfloat16 [64, 1536, 2560], P('gy', 'gx'), may hold values from -0.15625 to 0.15625
- shared_gate: bfloat16 [2560, 3072], P(None, 'gx'), may hold values from -0.125 to 0.125
- shared_up: bfloat16 [2560, 3072], P(None, 'gx'), may hold values from -0.125 to 0.125
- shared_down: bfloat16 [3072, 2560], P('gx'), may hold values from -0.109375 to 0.109375
- tree_kv: bfloat16 [8192, 1024], P(('gx', 'gy')), may hold values from -6 to 6
- accepted_path: int32 [256, 8], P(('gx', 'gy')), may hold values from 0 to 31, as said below
- accepted_len: int32 [256], P('gx'), may hold values from 1 to 8, as said below
- cache_owner: int32 [256], P('gx'), may hold values from 0 to 31, as said below
- owner_slot: int32 [256], P('gx'), may hold values from 0 to 8, as said below
Outputs:
- ffn_out: bfloat16 [8192, 2560], P(('gx', 'gy'))
- kept_kv: bfloat16 [4096, 1024], P(('gx', 'gy'))
Inputs may be any that keep to these rules, and one draw needn't show every extreme that they name: `expert_ids`: each row names 6 different experts; within the rows of one device no expert is named by more than 4 rows, and that number is reached. `accepted_path`: each row is a path from the tree's root: strictly increasing tree positions, the first one 0. Only the first accepted_len[r] positions of row r of accepted_path are kept; some request keeps all 8. `cache_owner`: A request's cache lies on the device with the same index of gx and this index of gy; each such device holds the caches of exactly 2 requests of its index of gx, or of none. Requests with the same owner have disjoint ranges owner_slot to owner_slot + 7, which together cover the owner's 16 rows.
All inputs are finite; a program needn't handle non-finite values.
Results may differ from a plain program's by a relative error of at most 0.015.
Values may be sent and summed in bfloat16 or wider, within the bound.
A program may use at most 128 MiB of HBM per device.

v0:
```python
import jax
import jax.numpy as jnp
from jax import lax
from jax.sharding import PartitionSpec as P

epsilon = 1e-05


def block_positions(dense, blocks, tok_rows):
    experts = dense.shape[1]
    routed = (dense > 0).reshape(blocks, tok_rows, experts).astype(jnp.int32)
    places = jnp.cumsum(routed, axis=1) - 1
    return places.reshape(blocks * tok_rows, experts)


def slot_sources(dense, blocks, tok_rows, capacity):
    experts = dense.shape[1]
    routed = (dense > 0).reshape(blocks, tok_rows, experts)
    places = block_positions(dense, blocks, tok_rows).reshape(blocks, tok_rows, experts)
    matched = routed[..., None] & (places[..., None] == jnp.arange(capacity, dtype=jnp.int32))
    within = jnp.arange(tok_rows, dtype=jnp.int32)[None, :, None, None]
    source = jnp.sum(jnp.where(matched, within, 0), axis=1)
    filled = jnp.any(matched, axis=1)
    source = source + (jnp.arange(blocks, dtype=jnp.int32) * tok_rows)[:, None, None]
    return (source, filled)


def pick_rows(row_table, source, filled):
    picked = jnp.take(row_table, source.reshape(-1), axis=0)
    picked = picked.reshape(source.shape + (row_table.shape[1],))
    return jnp.where(filled[..., None], picked, jnp.zeros((), row_table.dtype))


def weigh_slots(dense, flat_rows, blocks, tok_rows, top_count, capacity):
    experts = dense.shape[1]
    total_rows = blocks * tok_rows
    routed_all = dense > 0
    places = block_positions(dense, blocks, tok_rows)
    rank_all = jnp.cumsum(routed_all.astype(jnp.int32), axis=1) - 1
    listed = routed_all[:, None, :] & (
        rank_all[:, None, :] == jnp.arange(top_count, dtype=jnp.int32)[None, :, None]
    )
    which_expert = jnp.sum(jnp.where(listed, jnp.arange(experts, dtype=jnp.int32), 0), axis=-1)
    place_of = jnp.sum(jnp.where(listed, places[:, None, :], 0), axis=-1)
    weight_of = jnp.sum(
        jnp.where(listed, dense.astype(jnp.float32)[:, None, :], 0.0), axis=-1
    ).astype(jnp.bfloat16)
    block_of = jnp.arange(total_rows, dtype=jnp.int32) // tok_rows
    slot_of = (block_of[:, None] * experts + which_expert) * capacity + place_of
    fetched = jnp.take(flat_rows, slot_of.reshape(-1), axis=0).reshape(
        total_rows, top_count, flat_rows.shape[1]
    )
    return jnp.einsum("nk,nkd->nd", weight_of, fetched, preferred_element_type=jnp.float32)


def shards(
    hidden_in,
    norm_gain,
    router_weight,
    expert_ids,
    expert_gate,
    expert_up,
    expert_down,
    shared_gate,
    shared_up,
    shared_down,
    tree_kv,
    accepted_path,
    accepted_len,
    cache_owner,
    owner_slot,
):
    tok_rows = hidden_in.shape[0]
    model_width = hidden_in.shape[1]
    top_count = expert_ids.shape[1]
    experts = router_weight.shape[1]
    exp_local = expert_gate.shape[0]
    count_gx = lax.axis_size("gx")
    count_gy = lax.axis_size("gy")
    capacity = max(2, 4 * tok_rows * top_count // (3 * experts))
    widened = hidden_in.astype(jnp.float32)
    scale_inv = lax.rsqrt(jnp.mean(widened * widened, axis=-1, keepdims=True) + epsilon)
    normed = (widened * scale_inv * norm_gain).astype(jnp.bfloat16)
    scores = jax.nn.sigmoid(jnp.dot(normed, router_weight, preferred_element_type=jnp.float32))
    chosen = expert_ids[:, :, None] == jnp.arange(experts, dtype=jnp.int32)
    picked = jnp.sum(jnp.where(chosen, scores[:, None, :], 0.0), axis=-1)
    gate_values = (picked / jnp.sum(picked, axis=-1, keepdims=True)).astype(jnp.bfloat16)
    gate_dense = jnp.sum(
        jnp.where(chosen, gate_values.astype(jnp.float32)[:, :, None], 0.0), axis=1
    ).astype(jnp.bfloat16)
    normed_all, dense_all = (
        lax.all_gather(normed, "gx", axis=0, tiled=True),
        lax.all_gather(gate_dense, "gx", axis=0, tiled=True),
    )
    source, filled = slot_sources(dense_all, count_gx, tok_rows, capacity)
    outgoing = pick_rows(normed_all, source, filled).reshape(
        count_gx, count_gy, exp_local, capacity, model_width
    )
    slot_rows = lax.all_to_all(outgoing, "gy", split_axis=1, concat_axis=1, tiled=True)
    gate_out = jnp.einsum(
        "bjlcd,ldf->bjlcf", slot_rows, expert_gate, preferred_element_type=jnp.float32
    )
    up_out = jnp.einsum(
        "bjlcd,ldf->bjlcf", slot_rows, expert_up, preferred_element_type=jnp.float32
    )
    hidden = (jax.nn.silu(gate_out) * up_out).astype(jnp.bfloat16)
    partials = jnp.einsum(
        "bjlcf,lfd->bjlcd", hidden, expert_down, preferred_element_type=jnp.float32
    ).astype(jnp.bfloat16)
    requests = accepted_path.shape[0]
    accept_len = accepted_path.shape[1]
    tree_len = tok_rows // requests
    kv_width = tree_kv.shape[1]
    column = lax.axis_index("gy")
    local_req = jnp.arange(requests, dtype=jnp.int32)
    my_owner = jnp.take(cache_owner, column * requests + local_req)
    path_index = ((local_req * tree_len)[:, None] + accepted_path).reshape(-1)
    path_rows = jnp.take(tree_kv, path_index, axis=0).reshape(requests, accept_len, kv_width)
    to_owner = my_owner[None, :] == jnp.arange(count_gy, dtype=jnp.int32)[:, None]
    kv_leaving = jnp.where(
        to_owner[:, :, None, None], path_rows[None], jnp.zeros((), jnp.bfloat16)
    )[None]
    returned, kv_arrived = (
        lax.all_to_all(partials, "gy", split_axis=1, concat_axis=1, tiled=True),
        lax.all_to_all(kv_leaving, "gy", split_axis=1, concat_axis=1, tiled=True),
    )
    routed_part = weigh_slots(
        dense_all, returned.reshape(-1, model_width), count_gx, tok_rows, top_count, capacity
    )
    gate_out = jnp.dot(normed_all, shared_gate, preferred_element_type=jnp.float32)
    up_out = jnp.dot(normed_all, shared_up, preferred_element_type=jnp.float32)
    hidden = (jax.nn.silu(gate_out) * up_out).astype(jnp.bfloat16)
    term = jnp.dot(hidden, shared_down, preferred_element_type=jnp.float32)
    term = term + routed_part
    combined = lax.psum_scatter(term.astype(jnp.bfloat16), "gx", scatter_dimension=0, tiled=True)
    owner_rows = 2 * requests * accept_len
    steps_along = jnp.arange(accept_len, dtype=jnp.int32)
    owned_here = (cache_owner == column)[:, None] & (steps_along[None, :] < accepted_len[:, None])
    target = jnp.where(owned_here, owner_slot[:, None] + steps_along[None, :], owner_rows)
    kept_rows = jnp.zeros((owner_rows, kv_width), jnp.bfloat16)
    kept_rows = kept_rows.at[target.reshape(-1)].set(kv_arrived.reshape(-1, kv_width), mode="drop")
    return (combined, kept_rows)


def solution(mesh):
    in_specs = (
        P(("gx", "gy"), None),
        P(),
        P(),
        P(("gx", "gy"), None),
        P("gy", None, "gx"),
        P("gy", None, "gx"),
        P("gy", "gx", None),
        P(None, "gx"),
        P(None, "gx"),
        P("gx", None),
        P(("gx", "gy"), None),
        P(("gx", "gy"), None),
        P("gx"),
        P("gx"),
        P("gx"),
    )
    out_specs = (P(("gx", "gy"), None), P(("gx", "gy"), None))
    return jax.shard_map(shards, mesh=mesh, in_specs=in_specs, out_specs=out_specs, check_vma=False)
```

profile of v0, /device:TPU:2, one launch (start us, length us, event | category | flops | bytes accessed | tf_op | source)
XLA Modules:
  0.0 742.6 jit_solution(3152219275396013457)
XLA Ops:
  7.2 0.0 all-gather.2.cloned.1.call-start
  7.2 1.2 fusion.34
  8.4 1.7 fusion.36
  10.1 0.0 all-gather.2.cloned.1.call-update
  10.1 1.3 fusion.23
  11.4 1.0 select_reduce_fusion.4
  12.4 0.8 select_reduce_fusion.6
  13.2 13.3 %all_gather.7 = bf16[256,64]{1,0:T(8,128)(2,1)S(1)} all-gather(bf16[32,64]{1,0:T(8,128)(2,1)S(1)} %select_reduce_fusion.6), channel_id=1, replica_groups=mesh['gx'=8,'gy'=32] {'gx'}, dimensions={0}, use_global_device_ids=true | all-gather | bytes 36864 | tf_op jit(solution)/shard_map/all_gather | solution.py:93
  26.5 0.1 reduce-window_add_fusion
  26.7 0.2 select_reduce_fusion
  26.8 0.1 copy.97
  27.0 0.1 copy_add_fusion
  27.0 0.2 copy.101
  27.2 0.2 add.222
  27.4 0.1 copy.98
  27.5 0.1 compare_and_fusion
  27.6 0.3 copy.99
  27.9 0.1 fusion.27
  28.0 0.1 copy.95
  28.1 0.6 copy.96
  28.8 11.1 %all-gather.2.cloned.1.call-done = bf16[256,2560]{1,0:T(8,128)(2,1)} async-done(((bf16[32,2560]{1,0:T(8,128)(2,1)}), bf16[256,2560]{1,0:T(8,128)(2,1)}) %all-gather.2.cloned.1.call-update) | async-done | bytes 1310736 | tf_op jit(solution)/shard_map/all_gather | solution.py:92
  39.8 21.0 %gather_fusion = bf16[2048,2560]{1,0:T(8,128)(2,1)} fusion(bf16[256,2560]{1,0:T(8,128)(2,1)} %all-gather.2.cloned.1.call-done, s32[2048]{0:T(1024)S(1)} %broadcast_clamp_fusion), kind=kCustom, calls=%fused_computation | custom fusion | bytes 20979712 | tf_op jit(solution)/shard_map/jit(_take)/gather | solution.py:29
  60.8 17.8 %gather.21 = bf16[8,32,2,4,2560]{4,3,2,1,0:T(4,128)(2,1)} reshape(bf16[2048,2560]{1,0:T(8,128)(2,1)} %gather_fusion) | data formatting | bytes 20971520 | tf_op jit(solution)/shard_map/jit(_take)/gather | solution.py:29
  78.7 9.1 %select_select_fusion = bf16[8,32,2,4,2560]{4,3,2,1,0:T(4,128)(2,1)S(1)} fusion(bf16[8,32,2,4,2560]{4,3,2,1,0:T(4,128)(2,1)} %gather.21, pred[8,32,2,4]{3,2,1,0:T(4,128)(4,1)S(1)} %copy.99, pred[8,32,2,4]{3,2,1,0:T(4,128)(4,1)S(1)} %copy.96), kind=kLoop, calls=%fused_computation.7 | loop fusion | flops 10485760 | bytes 20975616 | tf_op jit(solution)/shard_map/jit(_where)/select_n | solution.py:31
  87.8 5.2 copy.102
  93.0 238.8 %all_to_all.15 = bf16[8,32,2,4,2560]{4,3,0,2,1:T(4,128)(2,1)S(1)} all-to-all(bf16[8,32,2,4,2560]{4,3,0,2,1:T(4,128)(2,1)S(1)} %copy.102), channel_id=1, replica_groups=mesh['gx'=8,'gy'=32] {'gy'}, dimensions={1} | all-to-all | bytes 20971520 | tf_op jit(solution)/shard_map/all_to_all | solution.py:99
  331.8 8.2 %fusion.3 = f32[2,8,32,4,192]{4,2,3,1,0:T(8,128)} fusion(bf16[8,32,2,4,2560]{4,3,0,2,1:T(4,128)(2,1)S(1)} %all_to_all.15, bf16[2,2560,192]{1,2,0:T(8,128)(2,1)S(1)} %copy-done.7), kind=kOutput, calls=%fused_computation.9 | convolution fusion | flops 2013265920 | bytes 14024704 | tf_op jit(solution)/shard_map/bjlcd,ldf->bjlcf/dot_general | solution.py:103
  340.0 8.0 %fusion.9 = bf16[8,32,2,4,192]{4,1,3,0,2:T(8,128)(2,1)S(1)} fusion(f32[2,8,32,4,192]{4,2,3,1,0:T(8,128)} %fusion.3, bf16[2,2560,192]{1,2,0:T(8,128)(2,1)} %param.19, bf16[8,32,2,4,2560]{4,3,0,2,1:T(4,128)(2,1)S(1)} %all_to_all.15), kind=kOutput, calls=%fused_computation.17 | convolution fusion | flops 2015625216 | bytes 14811136 | tf_op jit(solution)/shard_map/bjlcd,ldf->bjlcf/dot_general | solution.py:100
  348.0 3.1 convert_bitcast_fusion
  351.1 23.5 %copy.105 = bf16[8,32,2,4,2560]{4,3,0,2,1:T(4,128)(2,1)} copy(bf16[8,32,2,4,2560]{4,1,3,0,2:T(8,128)(2,1)S(1)} %convert_bitcast_fusion) | data formatting | bytes 20971520 | tf_op jit(solution)/shard_map/convert_element_type | solution.py:109
  374.6 7.9 %all-to-all-start.1 = ((bf16[8,32,2,4,2560]{4,3,0,2,1:T(4,128)(2,1)}), bf16[8,32,2,4,2560]{4,3,0,2,1:T(4,128)(2,1)}, u32[]{:S(2)}, u32[]{:S(2)}) async-start(bf16[8,32,2,4,2560]{4,3,0,2,1:T(4,128)(2,1)} %copy.105), calls=%async_computation.1 | async-start | bytes 20971520 | tf_op jit(solution)/shard_map/all_to_all | solution.py:124
  382.5 0.0 reduce-scatter.2.cloned.1.call-start
  382.6 0.7 convert_element_type.57
  383.2 0.1 copy.87
  383.3 0.7 copy.89
  384.1 1.0 copy.88
  385.0 0.1 copy.92
  385.1 0.1 reduce_window_sum.23
  385.3 0.1 select_reduce_fusion.2
  385.4 0.1 copy.107
  385.6 0.1 add.226
  385.7 0.2 copy.93
  385.9 0.8 convert_element_type.58
  386.7 0.1 select_reduce_fusion.3
  386.8 0.2 copy.111
  387.0 1.6 fusion.47
  388.6 229.1 %all-to-all-done.1 = bf16[8,32,2,4,2560]{4,3,0,2,1:T(4,128)(2,1)} async-done(((bf16[8,32,2,4,2560]{4,3,0,2,1:T(4,128)(2,1)}), bf16[8,32,2,4,2560]{4,3,0,2,1:T(4,128)(2,1)}, u32[]{:S(2)}, u32[]{:S(2)}) %all-to-all-start.1) | async-done | bytes 10485792 | tf_op jit(solution)/shard_map/all_to_all | solution.py:124
  617.7 10.1 %copy.106 = bf16[8,32,2,4,2560]{4,3,2,1,0:T(4,128)(2,1)} copy(bf16[8,32,2,4,2560]{4,3,0,2,1:T(4,128)(2,1)} %all-to-all-done.1) | data formatting | bytes 20971520 | tf_op jit(solution)/shard_map/all_to_all | solution.py:124
  627.8 17.1 %reshape.339 = bf16[2048,2560]{1,0:T(8,128)(2,1)} reshape(bf16[8,32,2,4,2560]{4,3,2,1,0:T(4,128)(2,1)} %copy.106) | data formatting | bytes 20971520 | tf_op jit(solution)/shard_map/reshape | solution.py:128
  644.9 20.4 %gather_fusion.1 = bf16[1536,2560]{1,0:T(8,128)(2,1)} fusion(bf16[2048,2560]{1,0:T(8,128)(2,1)} %reshape.339, s32[2048]{0:T(1024)S(1)} %pad_clamp_fusion), kind=kCustom, calls=%fused_computation.1 | custom fusion | bytes 15734784 | tf_op jit(solution)/shard_map/jit(_take)/gather | solution.py:50
  665.3 13.0 %gather.23 = bf16[256,6,2560]{2,1,0:T(8,128)(2,1)} reshape(bf16[1536,2560]{1,0:T(8,128)(2,1)} %gather_fusion.1) | data formatting | bytes 15728640 | tf_op jit(solution)/shard_map/jit(_take)/gather | solution.py:50
  678.3 8.5 %fusion = f32[256,1,2560]{2,1,0:T(1,128)} fusion(bf16[256,6,1]{1,2,0:T(2,128)(2,1)S(1)} %copy.111, bf16[256,6,2560]{2,1,0:T(8,128)(2,1)} %gather.23, pred[256,6]{1,0:T(8,128)(4,1)S(1)} %copy.93), kind=kOutput, calls=%fused_computation.4 | convolution fusion | flops 11796480 | bytes 10490368 | tf_op jit(solution)/shard_map/nk,nkd->nd/dot_general | solution.py:53
  686.8 5.9 fusion.8
  692.7 0.0 reduce-scatter.2.cloned.1.call-update
  692.8 0.6 dynamic-slice.2
  693.4 0.6 gather_fusion.2
  694.6 0.1 broadcast_select_fusion.1
  694.7 0.9 broadcast_select_fusion
  695.6 17.3 %all-to-all-start.2 = ((bf16[1,32,1,8,1024]{4,3,2,0,1:T(8,128)(2,1)}), bf16[1,32,1,8,1024]{4,3,2,0,1:T(8,128)(2,1)S(1)}, u32[]{:S(2)}, u32[]{:S(2)}) async-start(bf16[1,32,1,8,1024]{4,3,2,0,1:T(8,128)(2,1)} %broadcast_select_fusion), calls=%async_computation.3 | async-start | bytes 1048576 | tf_op jit(solution)/shard_map/all_to_all | solution.py:125
  713.0 0.1 add_select_fusion
  713.1 0.1 select_n.169
  713.2 14.7 %all-to-all-done.2 = bf16[1,32,1,8,1024]{4,3,2,0,1:T(8,128)(2,1)S(1)} async-done(((bf16[1,32,1,8,1024]{4,3,2,0,1:T(8,128)(2,1)}), bf16[1,32,1,8,1024]{4,3,2,0,1:T(8,128)(2,1)S(1)}, u32[]{:S(2)}, u32[]{:S(2)}) %all-to-all-start.2) | async-done | bytes 524320 | tf_op jit(solution)/shard_map/all_to_all | solution.py:125
  727.9 2.2 scatter_custom_fusion
  730.0 5.8 reduce-scatter.2.cloned.1.call-done
  (38 shorter events, 0.2 us)
Async XLA Ops:
  7.2 340.8 %copy-start = (bf16[2,192,2560]{2,1,0:T(8,128)(2,1)S(1)}, bf16[2,192,2560]{2,1,0:T(8,128)(2,1)}, u32[]{:S(2)}) copy-start(bf16[2,192,2560]{2,1,0:T(8,128)(2,1)} %param.21) | copy-start | bytes 5898244
  7.2 32.7 %all-gather.2.cloned.1.call-start = ((), (), s32[]{:S(2)}) async-start(), calls=%async_computation.4 | async-start | bytes 1474560 | tf_op jit(solution)/shard_map/all_gather | solution.py:92
  93.0 238.8 %copy-start.7 = (bf16[2,2560,192]{1,2,0:T(8,128)(2,1)S(1)}, bf16[2,2560,192]{1,2,0:T(8,128)(2,1)}, u32[]{:S(2)}) copy-start(bf16[2,2560,192]{1,2,0:T(8,128)(2,1)} %param.20) | copy-start | bytes 5898244
  374.6 12.4 %copy-start.2 = (bf16[256,2560]{1,0:T(8,128)(2,1)S(1)}, bf16[256,2560]{1,0:T(8,128)(2,1)}, u32[]{:S(2)}) copy-start(bf16[256,2560]{1,0:T(8,128)(2,1)} %all-gather.2.cloned.1.call-done) | copy-start | bytes 3932164
  374.6 12.4 %copy-start.3 = (bf16[2560,384]{1,0:T(8,128)(2,1)S(1)}, bf16[2560,384]{1,0:T(8,128)(2,1)}, u32[]{:S(2)}) copy-start(bf16[2560,384]{1,0:T(8,128)(2,1)} %param.22) | copy-start | bytes 5898244
  374.6 243.1 %all-to-all-start.1 = ((bf16[8,32,2,4,2560]{4,3,0,2,1:T(4,128)(2,1)}), bf16[8,32,2,4,2560]{4,3,0,2,1:T(4,128)(2,1)}, u32[]{:S(2)}, u32[]{:S(2)}) async-start(bf16[8,32,2,4,2560]{4,3,0,2,1:T(4,128)(2,1)} %copy.105), calls=%async_computation.1 | async-start | bytes 20971520 | tf_op jit(solution)/shard_map/all_to_all | solution.py:124
  382.5 353.3 %reduce-scatter.2.cloned.1.call-start = ((), (), s32[]{:S(2)}) async-start(), calls=%async_computation.5 | async-start | bytes 1474560 | tf_op jit(solution)/shard_map/reduce_scatter | solution.py:135
  686.8 5.9 copy-start.9
  686.8 6.5 copy-start.8
  686.8 6.5 copy-start.4
  686.8 49.0 %copy-start.1 = (bf16[2,192,2560]{2,1,0:T(8,128)(2,1)S(1)}, bf16[2,192,2560]{2,1,0:T(8,128)(2,1)}, u32[]{:S(2)}) copy-start(bf16[2,192,2560]{2,1,0:T(8,128)(2,1)} %param.21) | copy-start | bytes 5898244
  692.7 20.3 %copy-start.5 = (s32[32]{0:T(128)S(1)}, s32[32]{0:T(128)}, u32[]{:S(2)}) copy-start(s32[32]{0:T(128)} %param.29) | copy-start | bytes 388
  692.7 20.3 %copy-start.6 = (s32[32]{0:T(128)S(1)}, s32[32]{0:T(128)}, u32[]{:S(2)}) copy-start(s32[32]{0:T(128)} %param.27) | copy-start | bytes 388
  695.6 32.3 %all-to-all-start.2 = ((bf16[1,32,1,8,1024]{4,3,2,0,1:T(8,128)(2,1)}), bf16[1,32,1,8,1024]{4,3,2,0,1:T(8,128)(2,1)S(1)}, u32[]{:S(2)}, u32[]{:S(2)}) async-start(bf16[1,32,1,8,1024]{4,3,2,0,1:T(8,128)(2,1)} %broadcast_select_fusion), calls=%async_computation.3 | async-start | bytes 1048576 | tf_op jit(solution)/shard_map/all_to_all | solution.py:125
Sparse Core Ops, SparseCore 0:
  10.4 29.4 all-gather.1
  692.9 42.8 reduce-scatter.1
where the time goes:
time: 745 us; the launch traced here: 743 us
  waiting for transfers between devices  261 us (35%)
  blocking collectives  252 us (34%)
  local copies, waits for them, and re-layouts  136 us (18%)
  matrix products  36.5 us (5%)
  starting transfers between devices  25.4 us (3%)
  other arithmetic  17.3 us (2%)
  between operations  15.1 us (2%)
    all_to_all x1, blocking collectives, shards(): lax.all_to_all(outgoing, 'gy', split_axis=1, concat_axis=1, tiled=True)  239 us
    all_to_all x1, waiting for transfers between devices, shards(): lax.all_to_all(partials, 'gy', split_axis=1, concat_axis=1, tiled=True)  229 us
    gather x2, local copies, waits for them, and re-layouts, pick_rows(): picked = jnp.take(row_table, source.reshape(-1), axis=0)  38.8 us
    gather x2, local copies, waits for them, and re-layouts, weigh_slots(): jnp.take(flat_rows, slot_of.reshape(-1), axis=0)  33.5 us
    convert_element_type x1, local copies, waits for them, and re-layouts, shards(): partials = jnp.einsum('bjlcf,lfd->bjlcd', hidden, expert_down, preferred_...  23.5 us
    all_to_all x1, starting transfers between devices, shards(): lax.all_to_all(kv_leaving, 'gy', split_axis=1, concat_axis=1, tiled=True)  17.3 us
    reshape x1, local copies, waits for them, and re-layouts, shards(): returned.reshape(-1, model_width)  17.1 us
  transfers between devices with their start and end apart: 4, of which 4 were waited for; matrix products, arithmetic and copies ran while one was open for 2% of the time, Pallas kernels for 0%

commit v1 on v0

v1 whole, which is shorter than its diff:
```python
import jax
import jax.numpy as jnp
from jax import lax
from jax.experimental import pallas as pl
from jax.experimental.pallas import tpu as pltpu
from jax.sharding import PartitionSpec as P

NX, NY, NZ = 4, 4, 8
D = 2560
FFB = 192
SFB = 384
TOK = 32
EXPERTS = 64
META = 128
KVW = 1024
KVL = 256
ROW = D + META + KVL
COLS = 512
EPSILON = 1e-05
BF = jnp.bfloat16
F32 = jnp.float32
MESH = pl.DeviceIdType.MESH
COPIES = 128


def mm(a, b):
    return jnp.dot(a, b, preferred_element_type=F32)


def onehot(cond):
    return jnp.where(cond, 1.0, 0.0).astype(BF)


def iota(shape, dim):
    return lax.broadcasted_iota(jnp.int32, shape, dim)


def kernel(
    hidden, gain, router, ids, path, lens, owner, slot, tree,
    eg, eu, ed, sg, su, sd,
    out, kept,
    zbuf, xsend, ag, outb, rl, rs, sret, ret, ohg, comb, zl, zr,
    shb, outs, rls, rss, hid, hids, kvs, kvr,
    wg0, wu0, wd0, vg0, vu0, vd0, wg1, wu1, wd1, vg1, vu1, vd1,
    send_sem, recv_sem, local_sem,
):
    gx, gy = lax.axis_index("gx"), lax.axis_index("gy")
    y, c = gx // 2, gx % 2
    x, z = gy // NZ, gy % NZ
    zp = (gx, x * NZ + (z + 1) % NZ)
    zm = (gx, x * NZ + (z + NZ - 1) % NZ)
    xp = (gx, (x + 1) % NX * NZ + z)
    xm = (gx, (x + NX - 1) % NX * NZ + z)
    x2 = (gx, (x + 2) % NX * NZ + z)
    yp = ((y + 1) % NY * 2 + c, gy)
    ym = ((y + NY - 1) % NY * 2 + c, gy)
    mate = (y * 2 + 1 - c, gy)

    started = []

    def send(src, dst, device):
        number = len(started)
        copy = pltpu.make_async_remote_copy(
            src_ref=src, dst_ref=dst,
            send_sem=send_sem.at[number], recv_sem=recv_sem.at[number],
            device_id=device, device_id_type=MESH,
        )
        copy.start()
        started.append(copy)
        return copy

    own = []
    for k, (src, dst) in enumerate(
        ((sg, vg0), (su, vu0), (sd, vd0), (eg, wg0), (eu, wu0), (ed, wd0))
    ):
        copy = pltpu.make_async_copy(src, dst, local_sem.at[k])
        copy.start()
        own.append(copy)

    barrier = pltpu.get_barrier_semaphore()
    for device in (zp, zm, xp, xm, x2, yp, ym, mate):
        pl.semaphore_signal(barrier, inc=1, device_id=device, device_id_type=MESH)

    wide = hidden[...].astype(F32)
    scale = lax.rsqrt(jnp.mean(wide * wide, axis=-1, keepdims=True) + EPSILON)
    normed = (wide * scale * gain[...]).astype(BF)
    zbuf[0:TOK, 0:D] = normed
    shb[0:TOK, :] = normed
    scores = 1.0 / (1.0 + jnp.exp(-mm(normed, router[...])))
    lane = iota((TOK, EXPERTS), 1)
    chosen = lane == ids[:, 0:1]
    for k in range(1, ids.shape[1]):
        chosen = chosen | (lane == ids[:, k:k + 1])
    picked = jnp.where(chosen, scores, 0.0)
    gates = (picked / jnp.sum(picked, axis=-1, keepdims=True)).astype(BF)
    low = iota((EXPERTS, META), 1)
    high = iota((EXPERTS, META), 0)
    meta = mm(gates, onehot(low == high)) + mm(onehot(chosen), onehot(low == high + EXPERTS))
    zbuf[0:TOK, D:D + META] = meta.astype(BF)
    row = iota((TOK, 8), 0)
    steps = jnp.sum(
        jnp.where(row // 4 == iota((TOK, 8), 1), path[...].astype(F32), 0.0), axis=1, keepdims=True
    )
    square_row, square_lane = iota((TOK, TOK), 0), iota((TOK, TOK), 1)
    on_path = square_lane.astype(F32) == steps
    rows_kv = jnp.zeros((TOK, KVL), F32)
    for q in range(4):
        rows_kv += mm(onehot(on_path & (square_row % 4 == q)), tree[:, q * KVL:(q + 1) * KVL])
    zbuf[0:TOK, D + META:ROW] = rows_kv.astype(BF)

    pl.semaphore_wait(barrier, 8)

    right, left = {}, {}

    def hop(h):
        for ch in range(2):
            lo = ch * 16
            if h < 4 or ch == 0:
                if h > 1:
                    right[h - 1, ch].wait_recv()
                right[h, ch] = send(
                    zbuf.at[pl.ds((h - 1) * TOK + lo, 16), :], zbuf.at[pl.ds(h * TOK + lo, 16), :], zp
                )
            if h < 4 or ch == 1:
                if h > 1:
                    left[h - 1, ch].wait_recv()
                left[h, ch] = send(
                    zbuf.at[pl.ds((NZ - h + 1) % NZ * TOK + lo, 16), :],
                    zbuf.at[pl.ds((NZ - h) * TOK + lo, 16), :], zm,
                )

    hop(1)
    tokens = zbuf.at[pl.ds(0, TOK), pl.ds(0, D)]
    sh_p = send(tokens, shb.at[pl.ds(TOK, TOK), :], yp)
    sh_m = send(tokens, shb.at[pl.ds(2 * TOK, TOK), :], ym)
    other = [
        send(src, dst, mate)
        for src, dst in ((sg, vg1), (su, vu1), (sd, vd1), (eg, wg1), (eu, wu1), (ed, wd1))
    ]
    hop(2)
    sh_p.wait_recv()
    sh_p2 = send(shb.at[pl.ds(TOK, 16), :], shb.at[pl.ds(3 * TOK, 16), :], yp)
    sh_m.wait_recv()
    sh_m2 = send(shb.at[pl.ds(2 * TOK + 16, 16), :], shb.at[pl.ds(3 * TOK + 16, 16), :], ym)
    hop(3)
    hop(4)
    right[3, 1].wait_recv()
    left[3, 0].wait_recv()
    right[4, 0].wait_recv()
    left[4, 1].wait_recv()

    rows = NZ * TOK
    pair = iota((16, META), 0) % 8
    step = pair // 2
    turn = jnp.where(step == 2, 3, jnp.where(step == 3, 2, step))
    expert = 2 * ((x + turn) % NX * NZ + z) + pair % 2
    meta_lane = iota((16, META), 1)
    all_meta = zbuf[:, D:D + META]
    along = (((1,), (1,)), ((), ()))
    gate_of = lax.dot_general(onehot(meta_lane == expert), all_meta, along, preferred_element_type=F32)
    mask_of = lax.dot_general(
        onehot(meta_lane == expert + EXPERTS), all_meta, along, preferred_element_type=F32
    )
    big_row, big_lane = iota((rows, rows), 0), iota((rows, rows), 1)
    before = onehot((big_row < big_lane) & (big_row // TOK == big_lane // TOK))
    place = mm(mask_of.astype(BF), before)
    key = jnp.where(mask_of > 0.5, place, -1.0)
    slot_row, slot_lane = iota((TOK, rows), 0), iota((TOK, rows), 1)
    block = slot_lane // TOK == slot_row // 4
    seat = (slot_row % 4).astype(F32)

    def slots(i):
        parts = []
        for l in range(2):
            j = 2 * i + l
            here = block & (key[j:j + 1, :] == seat)
            ohg[pl.ds(j * TOK, TOK), :] = jnp.where(here, gate_of[j:j + 1, :], 0.0).astype(BF)
            parts.append(onehot(here))
        return jnp.concatenate(parts, axis=0)

    sent_x = {}
    for i, device in ((3, x2), (1, xp), (2, xm), (0, None)):
        table = slots(i)

        @pl.loop(0, D // COLS)
        def _(n):
            cols = pl.ds(pl.multiple_of(n * COLS, COLS), COLS)
            value = mm(table, zbuf[:, cols]).astype(BF)
            for l in range(2):
                part = value[l * TOK:(l + 1) * TOK, :]
                if i:
                    xsend[i - 1, l, :, cols] = part
                else:
                    ag[l, 0:TOK, cols] = part

        if i:
            for l in range(2):
                sent_x[i, l] = send(xsend.at[i - 1, l], ag.at[l, pl.ds(i * TOK, TOK), :], device)

    direct, relay = {}, {}

    def spread(j):
        for l in range(2):
            here = ag.at[l, pl.ds(j * TOK, TOK), :]
            direct[j, l, 0] = send(here, ag.at[l, pl.ds((NX + j) * TOK, TOK), :], yp)
            direct[j, l, 1] = send(here, ag.at[l, pl.ds((2 * NX + j) * TOK, TOK), :], ym)

    def pass_on(j):
        far = 3 * NX + j
        direct[j, 0, 0].wait_recv()
        relay[j, 0] = send(
            ag.at[0, pl.ds((NX + j) * TOK, TOK), :], ag.at[0, pl.ds(far * TOK, TOK), :], yp
        )
        direct[j, 1, 1].wait_recv()
        relay[j, 1] = send(
            ag.at[1, pl.ds((2 * NX + j) * TOK, TOK), :], ag.at[1, pl.ds(far * TOK, TOK), :], ym
        )

    spread(0)

    kv_row, kv_lane = iota((TOK, rows), 0), iota((TOK, rows), 1)
    spreader = onehot(kv_row == NZ * x + (z + NZ - kv_lane // TOK) % NZ)

    def per_lane(ref):
        return mm(jnp.broadcast_to(ref[...].astype(F32), (16, TOK)).astype(BF), spreader)[0:1, :]

    own_v, slot_v, len_v = per_lane(owner), per_lane(slot), per_lane(lens)
    pick_row, pick_lane = iota((64, rows), 0), iota((64, rows), 1)
    kv_step = pick_row // 16
    kv_turn = jnp.where(kv_step == 2, 3, jnp.where(kv_step == 3, 2, kv_step))
    target = ((x + kv_turn) % NX * NZ + z).astype(F32)
    depth = (pick_lane % TOK // 4).astype(F32)
    wanted = (own_v == target) & (slot_v + depth == (pick_row % 16).astype(F32)) & (depth < len_v)
    for q in range(4):
        value = mm(onehot(wanted & (pick_lane % 4 == q)), zbuf[:, D + META:ROW]).astype(BF)
        for i in range(4):
            kvs[i, :, q * KVL:(q + 1) * KVL] = value[i * 16:(i + 1) * 16, :]
    sent_kv = [
        send(kvs.at[i], kvr.at[i - 1], device) for i, device in ((1, xp), (2, xm), (3, x2))
    ]

    sh_p2.wait_recv()
    sh_m2.wait_recv()
    for k in range(3):
        own[k].wait()
        other[k].wait_recv()

    def silu_mul(g, u):
        return (g / (1.0 + jnp.exp(-g)) * u).astype(BF)

    for h, (vg, vu) in enumerate(((vg0, vu0), (vg1, vu1))):
        hids[h] = silu_mul(mm(shb[...], vg[...]), mm(shb[...], vu[...]))

    @pl.loop(0, D // COLS)
    def _(n):
        cols = pl.ds(pl.multiple_of(n * COLS, COLS), COLS)
        outs[:, cols] = (mm(hids[0], vd0[:, cols]) + mm(hids[1], vd1[:, cols])).astype(BF)

    far_p = send(outs.at[pl.ds(3 * TOK, 16), :], rls.at[0], yp)
    far_m = send(outs.at[pl.ds(3 * TOK + 16, 16), :], rls.at[1], ym)

    for l in range(2):
        sent_x[1, l].wait_recv()
    spread(1)
    pass_on(0)
    for l in range(2):
        sent_x[2, l].wait_recv()
    spread(2)
    pass_on(1)
    for l in range(2):
        sent_x[3, l].wait_recv()
    spread(3)
    far_p.wait_recv()
    outs[2 * TOK:2 * TOK + 16, :] = (
        outs[2 * TOK:2 * TOK + 16, :].astype(F32) + rls[0].astype(F32)
    ).astype(BF)
    far_m.wait_recv()
    outs[TOK + 16:2 * TOK, :] = (
        outs[TOK + 16:2 * TOK, :].astype(F32) + rls[1].astype(F32)
    ).astype(BF)
    back_p = send(outs.at[pl.ds(2 * TOK, TOK), :], rss.at[0], yp)
    back_m = send(outs.at[pl.ds(TOK, TOK), :], rss.at[1], ym)
    pass_on(2)
    pass_on(3)
    for k in range(3, 6):
        own[k].wait()
        other[k].wait_recv()
    for j in range(4):
        direct[j, 1, 0].wait_recv()
        direct[j, 0, 1].wait_recv()

    def routed(first, count):
        @pl.loop(0, 2)
        def _(l):
            for h, (wg, wu) in enumerate(((wg0, wu0), (wg1, wu1))):
                value = ag[l, first:first + count, :]
                hid[h, 0:count, :] = silu_mul(mm(value, wg[l]), mm(value, wu[l]))

            @pl.loop(0, D // COLS)
            def _(n):
                cols = pl.ds(pl.multiple_of(n * COLS, COLS), COLS)
                outb[l, first:first + count, cols] = (
                    mm(hid[0, 0:count, :], wd0[l, :, cols]) + mm(hid[1, 0:count, :], wd1[l, :, cols])
                ).astype(BF)

    span = NX * TOK
    routed(0, 3 * span)
    plain_p = send(outb.at[1, pl.ds(2 * span, span), :], rs.at[0, 1], yp)
    plain_m = send(outb.at[0, pl.ds(span, span), :], rs.at[1, 0], ym)
    for j in range(4):
        relay[j, 0].wait_recv()
        relay[j, 1].wait_recv()
    routed(3 * span, span)

    order = (3, 1, 2, 0)
    far = {}
    for j in order:
        rows_j = pl.ds(3 * span + j * TOK, TOK)
        far[j, 0] = send(outb.at[0, rows_j, :], rl.at[0, pl.ds(j * TOK, TOK), :], yp)
        far[j, 1] = send(outb.at[1, rows_j, :], rl.at[1, pl.ds(j * TOK, TOK), :], ym)
    back = {}
    sent_back = {}

    def add_far(j):
        lo = j * TOK
        for l, base, device in ((0, 2 * span, yp), (1, span, ym)):
            far[j, l].wait_recv()
            outb[l, base + lo:base + lo + TOK, :] = (
                outb[l, base + lo:base + lo + TOK, :].astype(F32) + rl[l, lo:lo + TOK, :].astype(F32)
            ).astype(BF)
            back[j, l] = send(
                outb.at[l, pl.ds(base + lo, TOK), :], rs.at[l, l, pl.ds(lo, TOK), :], device
            )

    def finish(j, device):
        lo = j * TOK
        for l in range(2):
            back[j, l].wait_recv()
        for l in range(2):
            total = (
                outb[l, lo:lo + TOK, :].astype(F32)
                + rs[0, l, lo:lo + TOK, :].astype(F32)
                + rs[1, l, lo:lo + TOK, :].astype(F32)
            ).astype(BF)
            if j:
                sret[l, lo:lo + TOK, :] = total
                sent_back[j, l] = send(
                    sret.at[l, pl.ds(lo, TOK), :], ret.at[pl.ds((2 * j + l) * TOK, TOK), :], device
                )
            else:
                ret[l * TOK:(l + 1) * TOK, :] = total

    goes = {0: None, 1: xm, 2: xp, 3: x2}
    add_far(3)
    plain_p.wait_recv()
    plain_m.wait_recv()
    add_far(1)
    finish(3, goes[3])
    add_far(2)
    finish(1, goes[1])
    add_far(0)
    finish(2, goes[2])
    finish(0, goes[0])
    for copy in sent_back.values():
        copy.wait_recv()

    across = (((0,), (0,)), ((), ()))

    def combine(k):
        weights = ohg[:, k * TOK:(k + 1) * TOK]

        @pl.loop(0, D // COLS)
        def _(n):
            cols = pl.ds(pl.multiple_of(n * COLS, COLS), COLS)
            comb[k * TOK:(k + 1) * TOK, cols] = lax.dot_general(
                weights, ret[:, cols], across, preferred_element_type=F32
            ).astype(BF)

    for k in range(NZ):
        combine(k)
    go_l, go_r = {}, {}
    for h in range(1, 5):
        for ch in range(2):
            lo = ch * 16
            for flow, going, buf, k, device in (
                (0, go_l, zl, 5 - h, zm), (1, go_r, zr, 3 + h, zp)
            ):
                if h == 1 and ch == flow:
                    continue
                at = k * TOK + lo
                if (h - 1, ch) in going:
                    going[h - 1, ch].wait_recv()
                    comb[at:at + 16, :] = (
                        comb[at:at + 16, :].astype(F32) + buf[h - 2, lo:lo + 16, :].astype(F32)
                    ).astype(BF)
                going[h, ch] = send(
                    comb.at[pl.ds(at, 16), :], buf.at[h - 1, pl.ds(lo, 16), :], device
                )

    back_p.wait_recv()
    back_m.wait_recv()
    for copy in sent_kv:
        copy.wait_recv()
    kept[...] = (
        kvs[0].astype(F32) + kvr[0].astype(F32) + kvr[1].astype(F32) + kvr[2].astype(F32)
    ).astype(BF)
    total = outs[0:TOK, :].astype(F32) + rss[0].astype(F32) + rss[1].astype(F32)
    total = total + comb[0:TOK, :].astype(F32)
    for ch in range(2):
        go_l[4, ch].wait_recv()
        go_r[4, ch].wait_recv()
    out[...] = (total + zl[3].astype(F32) + zr[3].astype(F32)).astype(BF)
    for copy in started:
        copy.wait_send()


def shards(
    hidden_in, norm_gain, router_weight, expert_ids, expert_gate, expert_up, expert_down,
    shared_gate, shared_up, shared_down, tree_kv, accepted_path, accepted_len, cache_owner, owner_slot,
):
    vmem = pl.BlockSpec(memory_space=pltpu.VMEM)
    hbm = pl.BlockSpec(memory_space=pl.ANY)
    V = pltpu.VMEM
    span = NX * TOK
    scratch = [
        V((NZ * TOK, ROW), BF),
        V((3, 2, TOK, D), BF),
        V((2, NY * span, D), BF),
        V((2, NY * span, D), BF),
        V((2, span, D), BF),
        V((2, 2, span, D), BF),
        V((2, span, D), BF),
        V((2 * span, D), BF),
        V((2 * span, NZ * TOK), BF),
        V((NZ * TOK, D), BF),
        V((4, TOK, D), BF),
        V((4, TOK, D), BF),
        V((NY * TOK, D), BF),
        V((NY * TOK, D), BF),
        V((2, 16, D), BF),
        V((2, TOK, D), BF),
        V((2, 3 * span, FFB), BF),
        V((2, NY * TOK, SFB), BF),
        V((4, 16, KVW), BF),
        V((3, 16, KVW), BF),
    ]
    for _ in range(2):
        scratch += [
            V((2, D, FFB), BF), V((2, D, FFB), BF), V((2, FFB, D), BF),
            V((D, SFB), BF), V((D, SFB), BF), V((SFB, D), BF),
        ]
    scratch += [
        pltpu.SemaphoreType.DMA((COPIES,)),
        pltpu.SemaphoreType.DMA((COPIES,)),
        pltpu.SemaphoreType.DMA((6,)),
    ]
    return pl.pallas_call(
        kernel,
        name="verify_ffn",
        out_shape=(
            jax.ShapeDtypeStruct((TOK, D), BF),
            jax.ShapeDtypeStruct((16, KVW), BF),
        ),
        in_specs=[vmem] * 9 + [hbm] * 6,
        out_specs=(vmem, vmem),
        scratch_shapes=scratch,
        compiler_params=pltpu.CompilerParams(
            collective_id=0, has_side_effects=True, vmem_limit_bytes=62 * 1024 * 1024
        ),
    )(
        hidden_in, norm_gain.reshape(1, D), router_weight, expert_ids, accepted_path,
        accepted_len.reshape(1, TOK), cache_owner.reshape(1, TOK), owner_slot.reshape(1, TOK), tree_kv,
        expert_gate, expert_up, expert_down, shared_gate, shared_up, shared_down,
    )


def solution(mesh):
    in_specs = (
        P(("gx", "gy"), None),
        P(),
        P(),
        P(("gx", "gy"), None),
        P("gy", None, "gx"),
        P("gy", None, "gx"),
        P("gy", "gx", None),
        P(None, "gx"),
        P(None, "gx"),
        P("gx", None),
        P(("gx", "gy"), None),
        P(("gx", "gy"), None),
        P("gx"),
        P("gx"),
        P("gx"),
    )
    out_specs = (P(("gx", "gy"), None), P(("gx", "gy"), None))
    return jax.shard_map(shards, mesh=mesh, in_specs=in_specs, out_specs=out_specs, check_vma=False)
```

time: 745 us -> 176 us (0.24)
  waiting for transfers between devices: 261 us -> 0 us
  blocking collectives: 252 us -> 0 us
  Pallas kernels: 0 us -> 160 us
  local copies, waits for them, and re-layouts: 136 us -> 14.7 us
  matrix products: 36.5 us -> 0 us
  starting transfers between devices: 25.4 us -> 0 us
  other arithmetic: 17.3 us -> 0 us
  between operations: 15.1 us -> 0.64 us
    all_to_all x2 -> x0, waiting for transfers between devices: 244 us -> none  [the longest x1 229 us: shards(): lax.all_to_all(partials, 'gy', split_axis=1, concat_axis=1, tiled=True)]
    all_to_all x1 -> x0, blocking collectives: 239 us -> none  [shards(): lax.all_to_all(outgoing, 'gy', split_axis=1, concat_axis=1, tiled=True)]
    pallas_call x0 -> x1, Pallas kernels: none -> 160 us  [shards(): pl.pallas_call(kernel, name='verify_ffn', out_shape=(jax.ShapeDtypeStruct...]
    gather x6 -> x0, local copies, waits for them, and re-layouts: 73.5 us -> none  [the longest x2 38.8 us: pick_rows(): picked = jnp.take(row_table, source.reshape(-1), axis=0)]
    dot_general x7 -> x0, matrix products: 36.5 us -> none  [the longest x1 8.48 us: weigh_slots(): jnp.einsum('nk,nkd->nd', weight_of, fetched, preferred_element_type=jnp.f...]
    all_to_all x2 -> x0, starting transfers between devices: 25.3 us -> none  [the longest x1 17.3 us: shards(): lax.all_to_all(kv_leaving, 'gy', split_axis=1, concat_axis=1, tiled=True)]
    convert_element_type x3 -> x0, local copies, waits for them, and re-layouts: 24.6 us -> none  [the longest x1 23.5 us: shards(): partials = jnp.einsum('bjlcf,lfd->bjlcd', hidden, expert_down, preferred_...]
    reshape x1, local copies, waits for them, and re-layouts: 17.1 us -> 1.31 us  [shards(): norm_gain.reshape(1, D)]
  transfers between devices with their start and end apart: 4 -> 0, of which waited for: 4 -> 0; matrix products, arithmetic and copies ran while one was open for 2% -> 0% of each run, Pallas kernels for 0% -> 0%
where the time goes in v1:
time: 176 us
  Pallas kernels  160 us (91%)
  local copies, waits for them, and re-layouts  14.7 us (8%)
    pallas_call x1, Pallas kernels, shards(): pl.pallas_call(kernel, name='verify_ffn', out_shape=(jax.ShapeDtypeStruct...  160 us
    unnamed x8, local copies, waits for them, and re-layouts  13.3 us

profile of v1, /device:TPU:2, one launch (start us, length us, event | category | flops | bytes accessed | tf_op | source)
XLA Modules:
  0.0 175.8 jit_solution(5879269017730234189)
XLA Ops:
  0.6 1.3 reshape.16.gain
  1.9 1.4 copy.18.ids
  3.3 2.1 %copy.17.router = bf16[2560,64]{1,0:T(8,128)(2,1)} copy(bf16[2560,64]{0,1:T(8,128)(2,1)} %param.17) | data formatting | bytes 655360 | tf_op args[2]
  5.4 0.0 copy-start
  5.4 4.4 %copy.19.eg = bf16[2,2560,192]{2,1,0:T(8,128)(2,1)} copy(bf16[2,2560,192]{1,2,0:T(8,128)(2,1)} %param.19) | data formatting | bytes 3932160 | tf_op args[4]
  9.8 0.0 copy-done
  9.8 2.5 %copy.20.eu = bf16[2,2560,192]{2,1,0:T(8,128)(2,1)} copy(bf16[2,2560,192]{1,2,0:T(8,128)(2,1)S(1)} %copy-done) | data formatting | bytes 3932160 | tf_op args[5]
  12.3 160.5 %verify_ffn.1 = (bf16[32,2560]{1,0:T(8,128)(2,1)}, bf16[16,1024]{1,0:T(8,128)(2,1)}) custom-call(bf16[32,2560]{1,0:T(8,128)(2,1)} %hidden.1, f32[1,2560]{1,0:T(1,128)} %reshape.16.gain, bf16[2560,64]{1,0:T(8,128)(2,1)} %copy.17.router, s32[32,6]{1,0:T(8,128)} %copy.18.ids, s32[1,8]{1,0:T(1,128)} %path.1, s32[1,32]{1,0:T(1,128)} %bitcast.3, s32[1,32]{1,0:T(1,128)} %bitcast.4, ...), custom_call_target="tpu_custom_call" | custom-call | tf_op jit(solution)/shard_map/verify_ffn/pallas_call | solution.py:457
  172.8 1.6 copy.23
  174.4 1.4 copy.24
Async XLA Ops:
  5.4 4.4 %copy-start = (bf16[2,2560,192]{1,2,0:T(8,128)(2,1)S(1)}, bf16[2,2560,192]{1,2,0:T(8,128)(2,1)}, u32[]{:S(2)}) copy-start(bf16[2,2560,192]{1,2,0:T(8,128)(2,1)} %param.20) | copy-start | bytes 5898244

commit v2 on v1

--- a/solution.py
+++ b/solution.py
@@ -27,6 +27,14 @@
     return jnp.dot(a, b, preferred_element_type=F32)
 
 
+def mm_nt(a, b):
+    return lax.dot_general(a, b, (((1,), (1,)), ((), ())), preferred_element_type=F32)
+
+
+def mm_tn(a, b):
+    return lax.dot_general(a, b, (((0,), (0,)), ((), ())), preferred_element_type=F32)
+
+
 def onehot(cond):
     return jnp.where(cond, 1.0, 0.0).astype(BF)
 
@@ -38,7 +46,7 @@
 def kernel(
     hidden, gain, router, ids, path, lens, owner, slot, tree,
     eg, eu, ed, sg, su, sd,
-    out, kept,
+    sums, moved,
     zbuf, xsend, ag, outb, rl, rs, sret, ret, ohg, comb, zl, zr,
     shb, outs, rls, rss, hid, hids, kvs, kvr,
     wg0, wu0, wd0, vg0, vu0, vd0, wg1, wu1, wd1, vg1, vu1, vd1,
@@ -83,19 +91,21 @@
 
     wide = hidden[...].astype(F32)
     scale = lax.rsqrt(jnp.mean(wide * wide, axis=-1, keepdims=True) + EPSILON)
-    normed = (wide * scale * gain[...]).astype(BF)
+    normed = (wide * scale * gain[...].reshape(1, D)).astype(BF)
     zbuf[0:TOK, 0:D] = normed
     shb[0:TOK, :] = normed
-    scores = 1.0 / (1.0 + jnp.exp(-mm(normed, router[...])))
-    lane = iota((TOK, EXPERTS), 1)
-    chosen = lane == ids[:, 0:1]
-    for k in range(1, ids.shape[1]):
-        chosen = chosen | (lane == ids[:, k:k + 1])
-    picked = jnp.where(chosen, scores, 0.0)
+    scores = 1.0 / (1.0 + jnp.exp(-mm_nt(normed, router[...])))
+    named = iota((EXPERTS, TOK), 0)
+    chosen = named == ids[0:1, :]
+    for k in range(1, ids.shape[0]):
+        chosen = chosen | (named == ids[k:k + 1, :])
+    chosen = onehot(chosen)
+    square = iota((EXPERTS, EXPERTS), 0) == iota((EXPERTS, EXPERTS), 1)
+    picked = jnp.where(mm_tn(chosen, onehot(square)) > 0.5, scores, 0.0)
     gates = (picked / jnp.sum(picked, axis=-1, keepdims=True)).astype(BF)
     low = iota((EXPERTS, META), 1)
     high = iota((EXPERTS, META), 0)
-    meta = mm(gates, onehot(low == high)) + mm(onehot(chosen), onehot(low == high + EXPERTS))
+    meta = mm(gates, onehot(low == high)) + mm_tn(chosen, onehot(low == high + EXPERTS))
     zbuf[0:TOK, D:D + META] = meta.astype(BF)
     row = iota((TOK, 8), 0)
     steps = jnp.sum(
@@ -156,11 +166,8 @@
     expert = 2 * ((x + turn) % NX * NZ + z) + pair % 2
     meta_lane = iota((16, META), 1)
     all_meta = zbuf[:, D:D + META]
-    along = (((1,), (1,)), ((), ()))
-    gate_of = lax.dot_general(onehot(meta_lane == expert), all_meta, along, preferred_element_type=F32)
-    mask_of = lax.dot_general(
-        onehot(meta_lane == expert + EXPERTS), all_meta, along, preferred_element_type=F32
-    )
+    gate_of = mm_nt(onehot(meta_lane == expert), all_meta)
+    mask_of = mm_nt(onehot(meta_lane == expert + EXPERTS), all_meta)
     big_row, big_lane = iota((rows, rows), 0), iota((rows, rows), 1)
     before = onehot((big_row < big_lane) & (big_row // TOK == big_lane // TOK))
     place = mm(mask_of.astype(BF), before)
@@ -294,7 +301,7 @@
         def _(l):
             for h, (wg, wu) in enumerate(((wg0, wu0), (wg1, wu1))):
                 value = ag[l, first:first + count, :]
-                hid[h, 0:count, :] = silu_mul(mm(value, wg[l]), mm(value, wu[l]))
+                hid[h, 0:count, :] = silu_mul(mm_nt(value, wg[l]), mm_nt(value, wu[l]))
 
             @pl.loop(0, D // COLS)
             def _(n):
@@ -364,17 +371,13 @@
     for copy in sent_back.values():
         copy.wait_recv()
 
-    across = (((0,), (0,)), ((), ()))
-
     def combine(k):
         weights = ohg[:, k * TOK:(k + 1) * TOK]
 
         @pl.loop(0, D // COLS)
         def _(n):
             cols = pl.ds(pl.multiple_of(n * COLS, COLS), COLS)
-            comb[k * TOK:(k + 1) * TOK, cols] = lax.dot_general(
-                weights, ret[:, cols], across, preferred_element_type=F32
-            ).astype(BF)
+            comb[k * TOK:(k + 1) * TOK, cols] = mm_tn(weights, ret[:, cols]).astype(BF)
 
     for k in range(NZ):
         combine(k)
@@ -401,7 +404,7 @@
     back_m.wait_recv()
     for copy in sent_kv:
         copy.wait_recv()
-    kept[...] = (
+    moved[...] = (
         kvs[0].astype(F32) + kvr[0].astype(F32) + kvr[1].astype(F32) + kvr[2].astype(F32)
     ).astype(BF)
     total = outs[0:TOK, :].astype(F32) + rss[0].astype(F32) + rss[1].astype(F32)
@@ -409,9 +412,14 @@
     for ch in range(2):
         go_l[4, ch].wait_recv()
         go_r[4, ch].wait_recv()
-    out[...] = (total + zl[3].astype(F32) + zr[3].astype(F32)).astype(BF)
+    sums[...] = (total + zl[3].astype(F32) + zr[3].astype(F32)).astype(BF)
     for copy in started:
         copy.wait_send()
+
+
+def place(sums, moved, out, kept):
+    out[...] = sums[...]
+    kept[...] = moved[...]
 
 
 def shards(
@@ -446,7 +454,7 @@
     ]
     for _ in range(2):
         scratch += [
-            V((2, D, FFB), BF), V((2, D, FFB), BF), V((2, FFB, D), BF),
+            V((2, FFB, D), BF), V((2, FFB, D), BF), V((2, FFB, D), BF),
             V((D, SFB), BF), V((D, SFB), BF), V((SFB, D), BF),
         ]
     scratch += [
@@ -454,7 +462,7 @@
         pltpu.SemaphoreType.DMA((COPIES,)),
         pltpu.SemaphoreType.DMA((6,)),
     ]
-    return pl.pallas_call(
+    sums, moved = pl.pallas_call(
         kernel,
         name="verify_ffn",
         out_shape=(
@@ -468,10 +476,20 @@
             collective_id=0, has_side_effects=True, vmem_limit_bytes=62 * 1024 * 1024
         ),
     )(
-        hidden_in, norm_gain.reshape(1, D), router_weight, expert_ids, accepted_path,
+        hidden_in, norm_gain, router_weight.T, expert_ids.T, accepted_path,
         accepted_len.reshape(1, TOK), cache_owner.reshape(1, TOK), owner_slot.reshape(1, TOK), tree_kv,
-        expert_gate, expert_up, expert_down, shared_gate, shared_up, shared_down,
+        expert_gate.swapaxes(1, 2), expert_up.swapaxes(1, 2), expert_down, shared_gate, shared_up, shared_down,
     )
+    return pl.pallas_call(
+        place,
+        name="place",
+        out_shape=(
+            jax.ShapeDtypeStruct((TOK, D), BF),
+            jax.ShapeDtypeStruct((16, KVW), BF),
+        ),
+        in_specs=[vmem] * 2,
+        out_specs=(vmem, vmem),
+    )(sums, moved)
 
 
 def solution(mesh):

time: 176 us -> 163 us (0.926)
  local copies, waits for them, and re-layouts: 14.7 us -> 0 us
  Pallas kernels: 160 us -> 162 us
    unnamed x8 -> x0, local copies, waits for them, and re-layouts: 13.3 us -> none
where the time goes in v2:
time: 163 us
  Pallas kernels  162 us (99%)
    pallas_call x1, Pallas kernels, shards(): pl.pallas_call(kernel, name='verify_ffn', out_shape=(jax.ShapeDtypeStruct...  161 us

profile of v2, /device:TPU:2, one launch (start us, length us, event | category | flops | bytes accessed | tf_op | source)
XLA Modules:
  0.0 162.8 jit_solution(646950992808009251)
XLA Ops:
  0.6 160.5 %verify_ffn.1 = (bf16[32,2560]{1,0:T(8,128)(2,1)}, bf16[16,1024]{1,0:T(8,128)(2,1)}) custom-call(bf16[32,2560]{1,0:T(8,128)(2,1)} %hidden.1, f32[2560]{0:T(1024)} %gain.1, bf16[64,2560]{1,0:T(8,128)(2,1)} %bitcast.9, s32[6,32]{1,0:T(8,128)} %bitcast.10, s32[1,8]{1,0:T(1,128)} %path.1, s32[1,32]{1,0:T(1,128)} %bitcast.11, s32[1,32]{1,0:T(1,128)} %bitcast.12, ...), custom_call_target="tpu_custom_call" | custom-call | tf_op jit(solution)/shard_map/verify_ffn/pallas_call | solution.py:465
  161.2 1.6 place.1

commit v3 on v2

--- a/solution.py
+++ b/solution.py
@@ -21,6 +21,7 @@
 F32 = jnp.float32
 MESH = pl.DeviceIdType.MESH
 COPIES = 128
+HALF = 128
 
 
 def mm(a, b):
@@ -33,6 +34,10 @@
 
 def mm_tn(a, b):
     return lax.dot_general(a, b, (((0,), (0,)), ((), ())), preferred_element_type=F32)
+
+
+def home(k):
+    return (k + 1) % NZ * TOK
 
 
 def onehot(cond):
@@ -92,7 +97,7 @@
     wide = hidden[...].astype(F32)
     scale = lax.rsqrt(jnp.mean(wide * wide, axis=-1, keepdims=True) + EPSILON)
     normed = (wide * scale * gain[...].reshape(1, D)).astype(BF)
-    zbuf[0:TOK, 0:D] = normed
+    zbuf[TOK:2 * TOK, 0:D] = normed
     shb[0:TOK, :] = normed
     scores = 1.0 / (1.0 + jnp.exp(-mm_nt(normed, router[...])))
     named = iota((EXPERTS, TOK), 0)
@@ -106,7 +111,7 @@
     low = iota((EXPERTS, META), 1)
     high = iota((EXPERTS, META), 0)
     meta = mm(gates, onehot(low == high)) + mm_tn(chosen, onehot(low == high + EXPERTS))
-    zbuf[0:TOK, D:D + META] = meta.astype(BF)
+    zbuf[TOK:2 * TOK, D:D + META] = meta.astype(BF)
     row = iota((TOK, 8), 0)
     steps = jnp.sum(
         jnp.where(row // 4 == iota((TOK, 8), 1), path[...].astype(F32), 0.0), axis=1, keepdims=True
@@ -116,7 +121,7 @@
     rows_kv = jnp.zeros((TOK, KVL), F32)
     for q in range(4):
         rows_kv += mm(onehot(on_path & (square_row % 4 == q)), tree[:, q * KVL:(q + 1) * KVL])
-    zbuf[0:TOK, D + META:ROW] = rows_kv.astype(BF)
+    zbuf[TOK:2 * TOK, D + META:ROW] = rows_kv.astype(BF)
 
     pl.semaphore_wait(barrier, 8)
 
@@ -129,18 +134,17 @@
                 if h > 1:
                     right[h - 1, ch].wait_recv()
                 right[h, ch] = send(
-                    zbuf.at[pl.ds((h - 1) * TOK + lo, 16), :], zbuf.at[pl.ds(h * TOK + lo, 16), :], zp
+                    zbuf.at[pl.ds(home(h - 1) + lo, 16), :], zbuf.at[pl.ds(home(h) + lo, 16), :], zp
                 )
             if h < 4 or ch == 1:
                 if h > 1:
                     left[h - 1, ch].wait_recv()
                 left[h, ch] = send(
-                    zbuf.at[pl.ds((NZ - h + 1) % NZ * TOK + lo, 16), :],
-                    zbuf.at[pl.ds((NZ - h) * TOK + lo, 16), :], zm,
+                    zbuf.at[pl.ds(home(1 - h) + lo, 16), :], zbuf.at[pl.ds(home(-h) + lo, 16), :], zm
                 )
 
     hop(1)
-    tokens = zbuf.at[pl.ds(0, TOK), pl.ds(0, D)]
+    tokens = shb.at[pl.ds(0, TOK), :]
     sh_p = send(tokens, shb.at[pl.ds(TOK, TOK), :], yp)
     sh_m = send(tokens, shb.at[pl.ds(2 * TOK, TOK), :], ym)
     other = [
@@ -153,80 +157,83 @@
     sh_m.wait_recv()
     sh_m2 = send(shb.at[pl.ds(2 * TOK + 16, 16), :], shb.at[pl.ds(3 * TOK + 16, 16), :], ym)
     hop(3)
-    hop(4)
-    right[3, 1].wait_recv()
-    left[3, 0].wait_recv()
-    right[4, 0].wait_recv()
-    left[4, 1].wait_recv()
-
-    rows = NZ * TOK
+
     pair = iota((16, META), 0) % 8
     step = pair // 2
     turn = jnp.where(step == 2, 3, jnp.where(step == 3, 2, step))
     expert = 2 * ((x + turn) % NX * NZ + z) + pair % 2
     meta_lane = iota((16, META), 1)
-    all_meta = zbuf[:, D:D + META]
-    gate_of = mm_nt(onehot(meta_lane == expert), all_meta)
-    mask_of = mm_nt(onehot(meta_lane == expert + EXPERTS), all_meta)
-    big_row, big_lane = iota((rows, rows), 0), iota((rows, rows), 1)
-    before = onehot((big_row < big_lane) & (big_row // TOK == big_lane // TOK))
-    place = mm(mask_of.astype(BF), before)
-    key = jnp.where(mask_of > 0.5, place, -1.0)
-    slot_row, slot_lane = iota((TOK, rows), 0), iota((TOK, rows), 1)
-    block = slot_lane // TOK == slot_row // 4
-    seat = (slot_row % 4).astype(F32)
-
-    def slots(i):
-        parts = []
-        for l in range(2):
-            j = 2 * i + l
-            here = block & (key[j:j + 1, :] == seat)
-            ohg[pl.ds(j * TOK, TOK), :] = jnp.where(here, gate_of[j:j + 1, :], 0.0).astype(BF)
-            parts.append(onehot(here))
-        return jnp.concatenate(parts, axis=0)
-
+    gate_pick = onehot(meta_lane == expert)
+    mask_pick = onehot(meta_lane == expert + EXPERTS)
+    sq_row, sq_lane = iota((HALF, HALF), 0), iota((HALF, HALF), 1)
+    before = onehot((sq_row < sq_lane) & (sq_row // TOK == sq_lane // TOK))
+    widen = onehot(iota((HALF, 16), 0) // 16 == iota((HALF, 16), 1))
+    block = sq_lane // TOK == sq_row % 16 // 4
+    seat = (sq_row % 4).astype(F32)
     sent_x = {}
-    for i, device in ((3, x2), (1, xp), (2, xm), (0, None)):
-        table = slots(i)
+
+    def slots(g):
+        base = g * HALF
+        all_meta = zbuf[base:base + HALF, D:D + META]
+        gate_of = mm_nt(gate_pick, all_meta).astype(BF)
+        mask_of = mm_nt(mask_pick, all_meta)
+        order = mm(mask_of.astype(BF), before)
+        key = mm(widen, jnp.where(mask_of > 0.5, order, -1.0).astype(BF))
+        here = block & (key == seat)
+        ohg[g] = jnp.where(here, mm(widen, gate_of), 0.0).T.astype(BF)
+        table = onehot(here)
 
         @pl.loop(0, D // COLS)
         def _(n):
             cols = pl.ds(pl.multiple_of(n * COLS, COLS), COLS)
-            value = mm(table, zbuf[:, cols]).astype(BF)
+            value = mm(table, zbuf[base:base + HALF, cols]).astype(BF)
             for l in range(2):
-                part = value[l * TOK:(l + 1) * TOK, :]
-                if i:
-                    xsend[i - 1, l, :, cols] = part
-                else:
-                    ag[l, 0:TOK, cols] = part
-
-        if i:
-            for l in range(2):
-                sent_x[i, l] = send(xsend.at[i - 1, l], ag.at[l, pl.ds(i * TOK, TOK), :], device)
+                ag[l, g * 256:g * 256 + 16, cols] = value[l * 16:(l + 1) * 16, :]
+            for j in range(2, 8):
+                xsend[g, j - 2, :, cols] = value[j * 16:(j + 1) * 16, :]
+
+        for i, device in ((3, x2), (1, xp), (2, xm)):
+            sent_x[g, i] = send(
+                xsend.at[g, pl.ds(2 * i - 2, 2)], ag.at[:, pl.ds(g * 256 + i * 16, 16), :], device
+            )
 
     direct, relay = {}, {}
 
-    def spread(j):
-        for l in range(2):
-            here = ag.at[l, pl.ds(j * TOK, TOK), :]
-            direct[j, l, 0] = send(here, ag.at[l, pl.ds((NX + j) * TOK, TOK), :], yp)
-            direct[j, l, 1] = send(here, ag.at[l, pl.ds((2 * NX + j) * TOK, TOK), :], ym)
-
-    def pass_on(j):
-        far = 3 * NX + j
-        direct[j, 0, 0].wait_recv()
-        relay[j, 0] = send(
-            ag.at[0, pl.ds((NX + j) * TOK, TOK), :], ag.at[0, pl.ds(far * TOK, TOK), :], yp
-        )
-        direct[j, 1, 1].wait_recv()
-        relay[j, 1] = send(
-            ag.at[1, pl.ds((2 * NX + j) * TOK, TOK), :], ag.at[1, pl.ds(far * TOK, TOK), :], ym
-        )
-
-    spread(0)
-
+    def spread(g, j):
+        if j:
+            sent_x[g, j].wait_recv()
+        at = g * 256 + j * 16
+        here = ag.at[:, pl.ds(at, 16), :]
+        direct[g, j, 0] = send(here, ag.at[:, pl.ds(at + 64, 16), :], yp)
+        direct[g, j, 1] = send(here, ag.at[:, pl.ds(at + 128, 16), :], ym)
+
+    def pass_on(g, j):
+        at = g * 256 + j * 16
+        for l, device in ((0, yp), (1, ym)):
+            direct[g, j, l].wait_recv()
+            relay[g, j, l] = send(
+                ag.at[l, pl.ds(at + 64 * (l + 1), 16), :], ag.at[l, pl.ds(at + 192, 16), :], device
+            )
+
+    slots(0)
+    spread(0, 0)
+    hop(4)
+    spread(0, 1)
+    spread(0, 2)
+    pass_on(0, 0)
+    right[3, 1].wait_recv()
+    left[3, 0].wait_recv()
+    right[4, 0].wait_recv()
+    left[4, 1].wait_recv()
+    slots(1)
+    spread(0, 3)
+    spread(1, 0)
+    pass_on(0, 1)
+    pass_on(0, 2)
+
+    rows = NZ * TOK
     kv_row, kv_lane = iota((TOK, rows), 0), iota((TOK, rows), 1)
-    spreader = onehot(kv_row == NZ * x + (z + NZ - kv_lane // TOK) % NZ)
+    spreader = onehot(kv_row == NZ * x + (z + NZ + 1 - kv_lane // TOK) % NZ)
 
     def per_lane(ref):
         return mm(jnp.broadcast_to(ref[...].astype(F32), (16, TOK)).astype(BF), spreader)[0:1, :]
@@ -266,17 +273,10 @@
     far_p = send(outs.at[pl.ds(3 * TOK, 16), :], rls.at[0], yp)
     far_m = send(outs.at[pl.ds(3 * TOK + 16, 16), :], rls.at[1], ym)
 
-    for l in range(2):
-        sent_x[1, l].wait_recv()
-    spread(1)
-    pass_on(0)
-    for l in range(2):
-        sent_x[2, l].wait_recv()
-    spread(2)
-    pass_on(1)
-    for l in range(2):
-        sent_x[3, l].wait_recv()
-    spread(3)
+    spread(1, 1)
+    spread(1, 2)
+    pass_on(0, 3)
+    spread(1, 3)
     far_p.wait_recv()
     outs[2 * TOK:2 * TOK + 16, :] = (
         outs[2 * TOK:2 * TOK + 16, :].astype(F32) + rls[0].astype(F32)
@@ -287,118 +287,136 @@
     ).astype(BF)
     back_p = send(outs.at[pl.ds(2 * TOK, TOK), :], rss.at[0], yp)
     back_m = send(outs.at[pl.ds(TOK, TOK), :], rss.at[1], ym)
-    pass_on(2)
-    pass_on(3)
     for k in range(3, 6):
         own[k].wait()
         other[k].wait_recv()
-    for j in range(4):
-        direct[j, 1, 0].wait_recv()
-        direct[j, 0, 1].wait_recv()
-
-    def routed(first, count):
+
+    def routed(g):
+        for j in range(4):
+            for l in range(2):
+                relay[g, j, l].wait_recv()
+
         @pl.loop(0, 2)
         def _(l):
             for h, (wg, wu) in enumerate(((wg0, wu0), (wg1, wu1))):
-                value = ag[l, first:first + count, :]
-                hid[h, 0:count, :] = silu_mul(mm_nt(value, wg[l]), mm_nt(value, wu[l]))
+                value = ag[l, g * 256:(g + 1) * 256, :]
+                hid[h] = silu_mul(mm_nt(value, wg[l]), mm_nt(value, wu[l]))
 
             @pl.loop(0, D // COLS)
             def _(n):
                 cols = pl.ds(pl.multiple_of(n * COLS, COLS), COLS)
-                outb[l, first:first + count, cols] = (
-                    mm(hid[0, 0:count, :], wd0[l, :, cols]) + mm(hid[1, 0:count, :], wd1[l, :, cols])
+                outb[l, g * 256:(g + 1) * 256, cols] = (
+                    mm(hid[0], wd0[l, :, cols]) + mm(hid[1], wd1[l, :, cols])
                 ).astype(BF)
 
-    span = NX * TOK
-    routed(0, 3 * span)
-    plain_p = send(outb.at[1, pl.ds(2 * span, span), :], rs.at[0, 1], yp)
-    plain_m = send(outb.at[0, pl.ds(span, span), :], rs.at[1, 0], ym)
-    for j in range(4):
-        relay[j, 0].wait_recv()
-        relay[j, 1].wait_recv()
-    routed(3 * span, span)
-
+    far, plain, back, sent_back = {}, {}, {}, {}
     order = (3, 1, 2, 0)
-    far = {}
-    for j in order:
-        rows_j = pl.ds(3 * span + j * TOK, TOK)
-        far[j, 0] = send(outb.at[0, rows_j, :], rl.at[0, pl.ds(j * TOK, TOK), :], yp)
-        far[j, 1] = send(outb.at[1, rows_j, :], rl.at[1, pl.ds(j * TOK, TOK), :], ym)
-    back = {}
-    sent_back = {}
-
-    def add_far(j):
-        lo = j * TOK
-        for l, base, device in ((0, 2 * span, yp), (1, span, ym)):
-            far[j, l].wait_recv()
-            outb[l, base + lo:base + lo + TOK, :] = (
-                outb[l, base + lo:base + lo + TOK, :].astype(F32) + rl[l, lo:lo + TOK, :].astype(F32)
+
+    def send_far(g):
+        for j in order:
+            at = pl.ds(g * 256 + 192 + j * 16, 16)
+            to = pl.ds(g * 64 + j * 16, 16)
+            far[g, j, 0] = send(outb.at[0, at, :], rl.at[0, to, :], yp)
+            far[g, j, 1] = send(outb.at[1, at, :], rl.at[1, to, :], ym)
+
+    def send_plain(g):
+        to = pl.ds(g * 64, 64)
+        plain[g, 0] = send(outb.at[1, pl.ds(g * 256 + 128, 64), :], rs.at[0, 1, to, :], yp)
+        plain[g, 1] = send(outb.at[0, pl.ds(g * 256 + 64, 64), :], rs.at[1, 0, to, :], ym)
+
+    def add_far(g, j):
+        lo = g * 64 + j * 16
+        for l, base, device in ((0, 128, yp), (1, 64, ym)):
+            far[g, j, l].wait_recv()
+            at = g * 256 + base + j * 16
+            outb[l, at:at + 16, :] = (
+                outb[l, at:at + 16, :].astype(F32) + rl[l, lo:lo + 16, :].astype(F32)
             ).astype(BF)
-            back[j, l] = send(
-                outb.at[l, pl.ds(base + lo, TOK), :], rs.at[l, l, pl.ds(lo, TOK), :], device
-            )
-
-    def finish(j, device):
-        lo = j * TOK
+            back[g, j, l] = send(outb.at[l, pl.ds(at, 16), :], rs.at[l, l, pl.ds(lo, 16), :], device)
+
+    goes = {1: xm, 2: xp, 3: x2}
+
+    def finish(g, j):
+        lo, at = g * 64 + j * 16, g * 256 + j * 16
         for l in range(2):
-            back[j, l].wait_recv()
+            back[g, j, l].wait_recv()
         for l in range(2):
             total = (
-                outb[l, lo:lo + TOK, :].astype(F32)
-                + rs[0, l, lo:lo + TOK, :].astype(F32)
-                + rs[1, l, lo:lo + TOK, :].astype(F32)
+                outb[l, at:at + 16, :].astype(F32)
+                + rs[0, l, lo:lo + 16, :].astype(F32)
+                + rs[1, l, lo:lo + 16, :].astype(F32)
             ).astype(BF)
             if j:
-                sret[l, lo:lo + TOK, :] = total
-                sent_back[j, l] = send(
-                    sret.at[l, pl.ds(lo, TOK), :], ret.at[pl.ds((2 * j + l) * TOK, TOK), :], device
-                )
+                sret[g, 2 * j - 2 + l] = total
             else:
-                ret[l * TOK:(l + 1) * TOK, :] = total
-
-    goes = {0: None, 1: xm, 2: xp, 3: x2}
-    add_far(3)
-    plain_p.wait_recv()
-    plain_m.wait_recv()
-    add_far(1)
-    finish(3, goes[3])
-    add_far(2)
-    finish(1, goes[1])
-    add_far(0)
-    finish(2, goes[2])
-    finish(0, goes[0])
-    for copy in sent_back.values():
-        copy.wait_recv()
-
-    def combine(k):
-        weights = ohg[:, k * TOK:(k + 1) * TOK]
+                ret[g, l] = total
+        if j:
+            sent_back[g, j] = send(
+                sret.at[g, pl.ds(2 * j - 2, 2)], ret.at[g, pl.ds(2 * j, 2)], goes[j]
+            )
+
+    def combine(g):
+        for j in (3, 1, 2):
+            sent_back[g, j].wait_recv()
+        weights = ohg[g]
 
         @pl.loop(0, D // COLS)
         def _(n):
             cols = pl.ds(pl.multiple_of(n * COLS, COLS), COLS)
-            comb[k * TOK:(k + 1) * TOK, cols] = mm_tn(weights, ret[:, cols]).astype(BF)
-
-    for k in range(NZ):
-        combine(k)
+            value = ret[g, :, :, cols].reshape(HALF, COLS)
+            comb[g * HALF:(g + 1) * HALF, cols] = mm(weights, value).astype(BF)
+
     go_l, go_r = {}, {}
-    for h in range(1, 5):
+
+    def fold(flow, h):
+        going, buf, k, device = (
+            (go_r, zr, 3 + h, zp) if flow else (go_l, zl, 5 - h, zm)
+        )
         for ch in range(2):
+            if h == 1 and ch == flow:
+                continue
             lo = ch * 16
-            for flow, going, buf, k, device in (
-                (0, go_l, zl, 5 - h, zm), (1, go_r, zr, 3 + h, zp)
-            ):
-                if h == 1 and ch == flow:
-                    continue
-                at = k * TOK + lo
-                if (h - 1, ch) in going:
-                    going[h - 1, ch].wait_recv()
-                    comb[at:at + 16, :] = (
-                        comb[at:at + 16, :].astype(F32) + buf[h - 2, lo:lo + 16, :].astype(F32)
-                    ).astype(BF)
-                going[h, ch] = send(
-                    comb.at[pl.ds(at, 16), :], buf.at[h - 1, pl.ds(lo, 16), :], device
-                )
+            at = home(k) + lo
+            if (h - 1, ch) in going:
+                going[h - 1, ch].wait_recv()
+                comb[at:at + 16, :] = (
+                    comb[at:at + 16, :].astype(F32) + buf[h - 2, lo:lo + 16, :].astype(F32)
+                ).astype(BF)
+            going[h, ch] = send(
+                comb.at[pl.ds(at, 16), :], buf.at[h - 1, pl.ds(lo, 16), :], device
+            )
+
+    routed(0)
+    send_far(0)
+    for j in range(4):
+        pass_on(1, j)
+    send_plain(0)
+    routed(1)
+    send_far(1)
+    send_plain(1)
+    for j in order:
+        add_far(1, j)
+    plain[0, 0].wait_recv()
+    plain[0, 1].wait_recv()
+    plain[1, 0].wait_recv()
+    plain[1, 1].wait_recv()
+    for j in order:
+        add_far(0, j)
+        finish(1, j)
+    combine(1)
+    fold(0, 1)
+    fold(1, 1)
+    finish(0, 3)
+    fold(0, 2)
+    fold(1, 2)
+    finish(0, 1)
+    finish(0, 2)
+    fold(1, 3)
+    finish(0, 0)
+    combine(0)
+    fold(0, 3)
+    fold(1, 4)
+    fold(0, 4)
 
     back_p.wait_recv()
     back_m.wait_recv()
@@ -408,7 +426,7 @@
         kvs[0].astype(F32) + kvr[0].astype(F32) + kvr[1].astype(F32) + kvr[2].astype(F32)
     ).astype(BF)
     total = outs[0:TOK, :].astype(F32) + rss[0].astype(F32) + rss[1].astype(F32)
-    total = total + comb[0:TOK, :].astype(F32)
+    total = total + comb[home(0):home(0) + TOK, :].astype(F32)
     for ch in range(2):
         go_l[4, ch].wait_recv()
         go_r[4, ch].wait_recv()
@@ -432,14 +450,14 @@
     span = NX * TOK
     scratch = [
         V((NZ * TOK, ROW), BF),
-        V((3, 2, TOK, D), BF),
+        V((2, 6, 16, D), BF),
         V((2, NY * span, D), BF),
         V((2, NY * span, D), BF),
         V((2, span, D), BF),
         V((2, 2, span, D), BF),
-        V((2, span, D), BF),
-        V((2 * span, D), BF),
-        V((2 * span, NZ * TOK), BF),
+        V((2, 6, 16, D), BF),
+        V((2, 8, 16, D), BF),
+        V((2, HALF, HALF), BF),
         V((NZ * TOK, D), BF),
         V((4, TOK, D), BF),
         V((4, TOK, D), BF),
@@ -447,7 +465,7 @@
         V((NY * TOK, D), BF),
         V((2, 16, D), BF),
         V((2, TOK, D), BF),
-        V((2, 3 * span, FFB), BF),
+        V((2, 2 * span, FFB), BF),
         V((2, NY * TOK, SFB), BF),
         V((4, 16, KVW), BF),
         V((3, 16, KVW), BF),

time: 163 us -> 141 us (0.87)
  Pallas kernels: 162 us -> 139 us
    pallas_call x1, Pallas kernels: 161 us -> 137 us  [shards(): pl.pallas_call(kernel, name='verify_ffn', out_shape=(jax.ShapeDtypeStruct...]
where the time goes in v3:
time: 141 us; the launch traced here: 140 us
  Pallas kernels  139 us (99%)
    pallas_call x1, Pallas kernels, shards(): pl.pallas_call(kernel, name='verify_ffn', out_shape=(jax.ShapeDtypeStruct...  137 us

profile of v3, /device:TPU:2, one launch (start us, length us, event | category | flops | bytes accessed | tf_op | source)
XLA Modules:
  0.0 139.6 jit_solution(6991839005114070805)
XLA Ops:
  0.6 137.3 %verify_ffn.1 = (bf16[32,2560]{1,0:T(8,128)(2,1)}, bf16[16,1024]{1,0:T(8,128)(2,1)}) custom-call(bf16[32,2560]{1,0:T(8,128)(2,1)} %hidden.1, f32[2560]{0:T(1024)} %gain.1, bf16[64,2560]{1,0:T(8,128)(2,1)} %bitcast.9, s32[6,32]{1,0:T(8,128)} %bitcast.10, s32[1,8]{1,0:T(1,128)} %path.1, s32[1,32]{1,0:T(1,128)} %bitcast.11, s32[1,32]{1,0:T(1,128)} %bitcast.12, ...), custom_call_target="tpu_custom_call" | custom-call | tf_op jit(solution)/shard_map/verify_ffn/pallas_call | solution.py:483
  138.0 1.6 %place.1 = (bf16[32,2560]{1,0:T(8,128)(2,1)}, bf16[16,1024]{1,0:T(8,128)(2,1)}) custom-call(bf16[32,2560]{1,0:T(8,128)(2,1)} %get-tuple-element.4.sums, bf16[16,1024]{1,0:T(8,128)(2,1)} %get-tuple-element.5.moved), custom_call_target="tpu_custom_call" | custom-call | tf_op jit(solution)/shard_map/place/pallas_call | solution.py:501

commit v4 on v3

--- a/solution.py
+++ b/solution.py
@@ -14,13 +14,16 @@
 META = 128
 KVW = 1024
 KVL = 256
-ROW = D + META + KVL
+KB = 768
+KA = D - KB
+ROW = KA + META + KVL
 COLS = 512
+PART = 256
 EPSILON = 1e-05
 BF = jnp.bfloat16
 F32 = jnp.float32
 MESH = pl.DeviceIdType.MESH
-COPIES = 128
+COPIES = 192
 HALF = 128
 
 
@@ -34,6 +37,10 @@
 
 def mm_tn(a, b):
     return lax.dot_general(a, b, (((0,), (0,)), ((), ())), preferred_element_type=F32)
+
+
+def place_of(k):
+    return (k + 1) % NZ
 
 
 def home(k):
@@ -54,6 +61,7 @@
     sums, moved,
     zbuf, xsend, ag, outb, rl, rs, sret, ret, ohg, comb, zl, zr,
     shb, outs, rls, rss, hid, hids, kvs, kvr,
+    zb, xsend_b, ret_b, comb_b, zl_b, zr_b, ohg_b,
     wg0, wu0, wd0, vg0, vu0, vd0, wg1, wu1, wd1, vg1, vu1, vd1,
     send_sem, recv_sem, local_sem,
 ):
@@ -97,8 +105,8 @@
     wide = hidden[...].astype(F32)
     scale = lax.rsqrt(jnp.mean(wide * wide, axis=-1, keepdims=True) + EPSILON)
     normed = (wide * scale * gain[...].reshape(1, D)).astype(BF)
-    zbuf[TOK:2 * TOK, 0:D] = normed
-    shb[0:TOK, :] = normed
+    zbuf[TOK:2 * TOK, 0:KA] = normed[:, 0:KA]
+    shb[0:TOK, 0:D] = normed
     scores = 1.0 / (1.0 + jnp.exp(-mm_nt(normed, router[...])))
     named = iota((EXPERTS, TOK), 0)
     chosen = named == ids[0:1, :]
@@ -111,7 +119,9 @@
     low = iota((EXPERTS, META), 1)
     high = iota((EXPERTS, META), 0)
     meta = mm(gates, onehot(low == high)) + mm_tn(chosen, onehot(low == high + EXPERTS))
-    zbuf[TOK:2 * TOK, D:D + META] = meta.astype(BF)
+    meta = meta.astype(BF)
+    zbuf[TOK:2 * TOK, KA:KA + META] = meta
+    shb[0:TOK, D:D + META] = meta
     row = iota((TOK, 8), 0)
     steps = jnp.sum(
         jnp.where(row // 4 == iota((TOK, 8), 1), path[...].astype(F32), 0.0), axis=1, keepdims=True
@@ -121,7 +131,7 @@
     rows_kv = jnp.zeros((TOK, KVL), F32)
     for q in range(4):
         rows_kv += mm(onehot(on_path & (square_row % 4 == q)), tree[:, q * KVL:(q + 1) * KVL])
-    zbuf[TOK:2 * TOK, D + META:ROW] = rows_kv.astype(BF)
+    zbuf[TOK:2 * TOK, KA + META:ROW] = rows_kv.astype(BF)
 
     pl.semaphore_wait(barrier, 8)
 
@@ -143,10 +153,23 @@
                     zbuf.at[pl.ds(home(1 - h) + lo, 16), :], zbuf.at[pl.ds(home(-h) + lo, 16), :], zm
                 )
 
+    right_b, left_b = {}, {}
+
+    def hop_b(h):
+        for ch in range(2):
+            part = pl.ds(2 * ch, 2)
+            if h < 4 or ch == 0:
+                if h > 1:
+                    right_b[h - 1, ch].wait_recv()
+                right_b[h, ch] = send(zb.at[place_of(h - 1), part], zb.at[place_of(h), part], zp)
+            if h < 4 or ch == 1:
+                if h > 1:
+                    left_b[h - 1, ch].wait_recv()
+                left_b[h, ch] = send(zb.at[place_of(1 - h), part], zb.at[place_of(-h), part], zm)
+
     hop(1)
-    tokens = shb.at[pl.ds(0, TOK), :]
-    sh_p = send(tokens, shb.at[pl.ds(TOK, TOK), :], yp)
-    sh_m = send(tokens, shb.at[pl.ds(2 * TOK, TOK), :], ym)
+    sh_p = send(shb.at[pl.ds(0, TOK), :], shb.at[pl.ds(TOK, TOK), :], yp)
+    sh_m = send(shb.at[pl.ds(0, TOK), :], shb.at[pl.ds(2 * TOK, TOK), :], ym)
     other = [
         send(src, dst, mate)
         for src, dst in ((sg, vg1), (su, vu1), (sd, vd1), (eg, wg1), (eu, wu1), (ed, wd1))
@@ -172,29 +195,56 @@
     seat = (sq_row % 4).astype(F32)
     sent_x = {}
 
-    def slots(g):
-        base = g * HALF
-        all_meta = zbuf[base:base + HALF, D:D + META]
+    def tables(all_meta):
         gate_of = mm_nt(gate_pick, all_meta).astype(BF)
         mask_of = mm_nt(mask_pick, all_meta)
         order = mm(mask_of.astype(BF), before)
         key = mm(widen, jnp.where(mask_of > 0.5, order, -1.0).astype(BF))
         here = block & (key == seat)
-        ohg[g] = jnp.where(here, mm(widen, gate_of), 0.0).T.astype(BF)
-        table = onehot(here)
-
-        @pl.loop(0, D // COLS)
+        return onehot(here), jnp.where(here, mm(widen, gate_of), 0.0).T.astype(BF)
+
+    def slots(g):
+        base = g * HALF
+        table, ohg[g] = tables(zbuf[base:base + HALF, KA:KA + META])
+
+        @pl.loop(0, KA // PART)
         def _(n):
-            cols = pl.ds(pl.multiple_of(n * COLS, COLS), COLS)
+            cols = pl.ds(pl.multiple_of(n * PART, PART), PART)
             value = mm(table, zbuf[base:base + HALF, cols]).astype(BF)
             for l in range(2):
-                ag[l, g * 256:g * 256 + 16, cols] = value[l * 16:(l + 1) * 16, :]
+                ag[l, 4 * g, 0:16, cols] = value[l * 16:(l + 1) * 16, :]
             for j in range(2, 8):
                 xsend[g, j - 2, :, cols] = value[j * 16:(j + 1) * 16, :]
 
         for i, device in ((3, x2), (1, xp), (2, xm)):
             sent_x[g, i] = send(
-                xsend.at[g, pl.ds(2 * i - 2, 2)], ag.at[:, pl.ds(g * 256 + i * 16, 16), :], device
+                xsend.at[g, pl.ds(2 * i - 2, 2)],
+                ag.at[:, 4 * g, pl.ds(i * 16, 16), pl.ds(0, KA)], device,
+            )
+
+    sent_xb = {}
+
+    def slots_b(g):
+        homes = slice(4 * g, 4 * g + 4)
+
+        @pl.loop(0, NY)
+        def _(r):
+            table, ohg_b[g, r] = tables(zb[homes, r, :, KB:KB + META].reshape(HALF, META))
+
+            @pl.loop(0, KB // PART)
+            def _(n):
+                at = pl.multiple_of(n * PART, PART)
+                cols = pl.ds(at, PART)
+                value = mm(table, zb[homes, r, :, cols].reshape(HALF, PART)).astype(BF)
+                for l in range(2):
+                    ag[l, 4 * g + r, 0:16, pl.ds(KA + at, PART)] = value[l * 16:(l + 1) * 16, :]
+                for j in range(2, 8):
+                    xsend_b[g, j - 2, r, :, cols] = value[j * 16:(j + 1) * 16, :]
+
+        for i, device in ((3, x2), (1, xp), (2, xm)):
+            sent_xb[g, i] = send(
+                xsend_b.at[g, pl.ds(2 * i - 2, 2)],
+                ag.at[:, pl.ds(4 * g, 4), pl.ds(i * 16, 16), pl.ds(KA, KB)], device,
             )
 
     direct, relay = {}, {}
@@ -202,22 +252,27 @@
     def spread(g, j):
         if j:
             sent_x[g, j].wait_recv()
-        at = g * 256 + j * 16
-        here = ag.at[:, pl.ds(at, 16), :]
-        direct[g, j, 0] = send(here, ag.at[:, pl.ds(at + 64, 16), :], yp)
-        direct[g, j, 1] = send(here, ag.at[:, pl.ds(at + 128, 16), :], ym)
+        at, cols = pl.ds(j * 16, 16), pl.ds(0, KA)
+        here = ag.at[:, 4 * g, at, cols]
+        direct[g, j, 0] = send(here, ag.at[:, 4 * g + 1, at, cols], yp)
+        direct[g, j, 1] = send(here, ag.at[:, 4 * g + 2, at, cols], ym)
 
     def pass_on(g, j):
-        at = g * 256 + j * 16
+        at, cols = pl.ds(j * 16, 16), pl.ds(0, KA)
         for l, device in ((0, yp), (1, ym)):
             direct[g, j, l].wait_recv()
             relay[g, j, l] = send(
-                ag.at[l, pl.ds(at + 64 * (l + 1), 16), :], ag.at[l, pl.ds(at + 192, 16), :], device
+                ag.at[l, 4 * g + l + 1, at, cols], ag.at[l, 4 * g + 3, at, cols], device
             )
 
     slots(0)
     spread(0, 0)
     hop(4)
+    sh_p2.wait_recv()
+    sh_m2.wait_recv()
+    for r in range(NY):
+        zb[place_of(0), r] = shb[r * TOK:(r + 1) * TOK, KA:D + META]
+    hop_b(1)
     spread(0, 1)
     spread(0, 2)
     pass_on(0, 0)
@@ -228,8 +283,16 @@
     slots(1)
     spread(0, 3)
     spread(1, 0)
+    hop_b(2)
     pass_on(0, 1)
     pass_on(0, 2)
+    hop_b(3)
+    slots_b(0)
+    spread(1, 1)
+    spread(1, 2)
+    pass_on(0, 3)
+    spread(1, 3)
+    hop_b(4)
 
     rows = NZ * TOK
     kv_row, kv_lane = iota((TOK, rows), 0), iota((TOK, rows), 1)
@@ -246,15 +309,13 @@
     depth = (pick_lane % TOK // 4).astype(F32)
     wanted = (own_v == target) & (slot_v + depth == (pick_row % 16).astype(F32)) & (depth < len_v)
     for q in range(4):
-        value = mm(onehot(wanted & (pick_lane % 4 == q)), zbuf[:, D + META:ROW]).astype(BF)
+        value = mm(onehot(wanted & (pick_lane % 4 == q)), zbuf[:, KA + META:ROW]).astype(BF)
         for i in range(4):
             kvs[i, :, q * KVL:(q + 1) * KVL] = value[i * 16:(i + 1) * 16, :]
     sent_kv = [
         send(kvs.at[i], kvr.at[i - 1], device) for i, device in ((1, xp), (2, xm), (3, x2))
     ]
 
-    sh_p2.wait_recv()
-    sh_m2.wait_recv()
     for k in range(3):
         own[k].wait()
         other[k].wait_recv()
@@ -263,30 +324,45 @@
         return (g / (1.0 + jnp.exp(-g)) * u).astype(BF)
 
     for h, (vg, vu) in enumerate(((vg0, vu0), (vg1, vu1))):
-        hids[h] = silu_mul(mm(shb[...], vg[...]), mm(shb[...], vu[...]))
+        hids[h] = silu_mul(mm(shb[:, 0:D], vg[...]), mm(shb[:, 0:D], vu[...]))
 
     @pl.loop(0, D // COLS)
     def _(n):
         cols = pl.ds(pl.multiple_of(n * COLS, COLS), COLS)
         outs[:, cols] = (mm(hids[0], vd0[:, cols]) + mm(hids[1], vd1[:, cols])).astype(BF)
 
-    far_p = send(outs.at[pl.ds(3 * TOK, 16), :], rls.at[0], yp)
-    far_m = send(outs.at[pl.ds(3 * TOK + 16, 16), :], rls.at[1], ym)
-
-    spread(1, 1)
-    spread(1, 2)
-    pass_on(0, 3)
-    spread(1, 3)
-    far_p.wait_recv()
-    outs[2 * TOK:2 * TOK + 16, :] = (
-        outs[2 * TOK:2 * TOK + 16, :].astype(F32) + rls[0].astype(F32)
-    ).astype(BF)
-    far_m.wait_recv()
-    outs[TOK + 16:2 * TOK, :] = (
-        outs[TOK + 16:2 * TOK, :].astype(F32) + rls[1].astype(F32)
-    ).astype(BF)
-    back_p = send(outs.at[pl.ds(2 * TOK, TOK), :], rss.at[0], yp)
-    back_m = send(outs.at[pl.ds(TOK, TOK), :], rss.at[1], ym)
+    def shared_far(cols):
+        return (
+            send(outs.at[pl.ds(3 * TOK, 16), cols], rls.at[0, :, cols], yp),
+            send(outs.at[pl.ds(3 * TOK + 16, 16), cols], rls.at[1, :, cols], ym),
+        )
+
+    def shared_back(parts, cols):
+        parts[0].wait_recv()
+        outs[2 * TOK:2 * TOK + 16, cols] = (
+            outs[2 * TOK:2 * TOK + 16, cols].astype(F32) + rls[0, :, cols].astype(F32)
+        ).astype(BF)
+        parts[1].wait_recv()
+        outs[TOK + 16:2 * TOK, cols] = (
+            outs[TOK + 16:2 * TOK, cols].astype(F32) + rls[1, :, cols].astype(F32)
+        ).astype(BF)
+        return (
+            send(outs.at[pl.ds(2 * TOK, TOK), cols], rss.at[0, :, cols], yp),
+            send(outs.at[pl.ds(TOK, TOK), cols], rss.at[1, :, cols], ym),
+        )
+
+    cols_a, cols_b = pl.ds(0, KA), pl.ds(KA, KB)
+    shared_a = shared_far(cols_a)
+    pass_on(1, 0)
+    pass_on(1, 1)
+    right_b[3, 1].wait_recv()
+    left_b[3, 0].wait_recv()
+    right_b[4, 0].wait_recv()
+    left_b[4, 1].wait_recv()
+    slots_b(1)
+    shared_a = shared_back(shared_a, cols_a)
+    pass_on(1, 2)
+    pass_on(1, 3)
     for k in range(3, 6):
         own[k].wait()
         other[k].wait_recv()
@@ -295,54 +371,57 @@
         for j in range(4):
             for l in range(2):
                 relay[g, j, l].wait_recv()
+        for i in (3, 1, 2):
+            sent_xb[g, i].wait_recv()
 
         @pl.loop(0, 2)
         def _(l):
             for h, (wg, wu) in enumerate(((wg0, wu0), (wg1, wu1))):
-                value = ag[l, g * 256:(g + 1) * 256, :]
+                value = ag[l, 4 * g:4 * g + 4].reshape(256, D)
                 hid[h] = silu_mul(mm_nt(value, wg[l]), mm_nt(value, wu[l]))
 
             @pl.loop(0, D // COLS)
             def _(n):
                 cols = pl.ds(pl.multiple_of(n * COLS, COLS), COLS)
-                outb[l, g * 256:(g + 1) * 256, cols] = (
+                outb[l, 4 * g:4 * g + 4, :, cols] = (
                     mm(hid[0], wd0[l, :, cols]) + mm(hid[1], wd1[l, :, cols])
-                ).astype(BF)
+                ).astype(BF).reshape(4, 64, COLS)
 
     far, plain, back, sent_back = {}, {}, {}, {}
     order = (3, 1, 2, 0)
 
     def send_far(g):
         for j in order:
-            at = pl.ds(g * 256 + 192 + j * 16, 16)
+            at = pl.ds(j * 16, 16)
             to = pl.ds(g * 64 + j * 16, 16)
-            far[g, j, 0] = send(outb.at[0, at, :], rl.at[0, to, :], yp)
-            far[g, j, 1] = send(outb.at[1, at, :], rl.at[1, to, :], ym)
+            far[g, j, 0] = send(outb.at[0, 4 * g + 3, at, cols_a], rl.at[0, to, :], yp)
+            far[g, j, 1] = send(outb.at[1, 4 * g + 3, at, cols_a], rl.at[1, to, :], ym)
 
     def send_plain(g):
         to = pl.ds(g * 64, 64)
-        plain[g, 0] = send(outb.at[1, pl.ds(g * 256 + 128, 64), :], rs.at[0, 1, to, :], yp)
-        plain[g, 1] = send(outb.at[0, pl.ds(g * 256 + 64, 64), :], rs.at[1, 0, to, :], ym)
+        plain[g, 0] = send(outb.at[1, 4 * g + 2, :, cols_a], rs.at[0, 1, to, :], yp)
+        plain[g, 1] = send(outb.at[0, 4 * g + 1, :, cols_a], rs.at[1, 0, to, :], ym)
 
     def add_far(g, j):
-        lo = g * 64 + j * 16
-        for l, base, device in ((0, 128, yp), (1, 64, ym)):
+        lo, at = g * 64 + j * 16, j * 16
+        for l, r, device in ((0, 2, yp), (1, 1, ym)):
             far[g, j, l].wait_recv()
-            at = g * 256 + base + j * 16
-            outb[l, at:at + 16, :] = (
-                outb[l, at:at + 16, :].astype(F32) + rl[l, lo:lo + 16, :].astype(F32)
+            outb[l, 4 * g + r, at:at + 16, 0:KA] = (
+                outb[l, 4 * g + r, at:at + 16, 0:KA].astype(F32) + rl[l, lo:lo + 16, :].astype(F32)
             ).astype(BF)
-            back[g, j, l] = send(outb.at[l, pl.ds(at, 16), :], rs.at[l, l, pl.ds(lo, 16), :], device)
+            back[g, j, l] = send(
+                outb.at[l, 4 * g + r, pl.ds(at, 16), cols_a], rs.at[l, l, pl.ds(lo, 16), :], device
+            )
 
     goes = {1: xm, 2: xp, 3: x2}
 
     def finish(g, j):
-        lo, at = g * 64 + j * 16, g * 256 + j * 16
+        lo, at = g * 64 + j * 16, j * 16
         for l in range(2):
             back[g, j, l].wait_recv()
         for l in range(2):
             total = (
-                outb[l, at:at + 16, :].astype(F32)
+                outb[l, 4 * g, at:at + 16, 0:KA].astype(F32)
                 + rs[0, l, lo:lo + 16, :].astype(F32)
                 + rs[1, l, lo:lo + 16, :].astype(F32)
             ).astype(BF)
@@ -355,16 +434,59 @@
                 sret.at[g, pl.ds(2 * j - 2, 2)], ret.at[g, pl.ds(2 * j, 2)], goes[j]
             )
 
+    back_b = {}
+
+    def return_b(g):
+        for j in order[:3]:
+            back_b[g, j] = send(
+                outb.at[:, pl.ds(4 * g, 4), pl.ds(j * 16, 16), cols_b], ret_b.at[g, pl.ds(2 * j, 2)], goes[j]
+            )
+        ret_b[g, 0:2] = outb[:, 4 * g:4 * g + 4, 0:16, KA:D]
+
     def combine(g):
         for j in (3, 1, 2):
             sent_back[g, j].wait_recv()
         weights = ohg[g]
 
-        @pl.loop(0, D // COLS)
+        @pl.loop(0, KA // PART)
         def _(n):
-            cols = pl.ds(pl.multiple_of(n * COLS, COLS), COLS)
-            value = ret[g, :, :, cols].reshape(HALF, COLS)
+            cols = pl.ds(pl.multiple_of(n * PART, PART), PART)
+            value = ret[g, :, :, cols].reshape(HALF, PART)
             comb[g * HALF:(g + 1) * HALF, cols] = mm(weights, value).astype(BF)
+
+    def combine_b(g):
+        for j in (3, 1, 2):
+            back_b[g, j].wait_recv()
+
+        @pl.loop(0, NY)
+        def _(r):
+            weights = ohg_b[g, r]
+
+            @pl.loop(0, KB // PART)
+            def _(n):
+                cols = pl.ds(pl.multiple_of(n * PART, PART), PART)
+                value = ret_b[g, :, r, :, cols].reshape(HALF, PART)
+                comb_b[4 * g:4 * g + 4, r, :, cols] = (
+                    mm(weights, value).astype(BF).reshape(4, TOK, PART)
+                )
+
+    go_lb, go_rb = {}, {}
+
+    def fold_b(flow, h):
+        going, buf, k, device = (
+            (go_rb, zr_b, 3 + h, zp) if flow else (go_lb, zl_b, 5 - h, zm)
+        )
+        m = place_of(k)
+        for ch in range(2):
+            if h == 1 and ch == flow:
+                continue
+            part = pl.ds(2 * ch, 2)
+            if (h - 1, ch) in going:
+                going[h - 1, ch].wait_recv()
+                comb_b[m, part] = (
+                    comb_b[m, part].astype(F32) + buf[h - 2, part].astype(F32)
+                ).astype(BF)
+            going[h, ch] = send(comb_b.at[m, part], buf.at[h - 1, part], device)
 
     go_l, go_r = {}, {}
 
@@ -387,50 +509,77 @@
             )
 
     routed(0)
+    return_b(0)
     send_far(0)
-    for j in range(4):
-        pass_on(1, j)
     send_plain(0)
     routed(1)
+    return_b(1)
     send_far(1)
     send_plain(1)
+    combine_b(0)
     for j in order:
         add_far(1, j)
-    plain[0, 0].wait_recv()
-    plain[0, 1].wait_recv()
-    plain[1, 0].wait_recv()
-    plain[1, 1].wait_recv()
     for j in order:
         add_far(0, j)
-        finish(1, j)
+    combine_b(1)
+    fold_b(0, 1)
+    fold_b(1, 1)
+    for g in range(2):
+        for k in range(2):
+            plain[g, k].wait_recv()
+    finish(1, 3)
+    finish(1, 1)
+    fold_b(0, 2)
+    fold_b(1, 2)
+    finish(1, 2)
+    finish(1, 0)
     combine(1)
     fold(0, 1)
     fold(1, 1)
+    fold_b(0, 3)
+    fold_b(1, 3)
     finish(0, 3)
+    finish(0, 1)
     fold(0, 2)
     fold(1, 2)
-    finish(0, 1)
     finish(0, 2)
+    finish(0, 0)
+    fold_b(0, 4)
+    fold_b(1, 4)
     fold(1, 3)
-    finish(0, 0)
     combine(0)
     fold(0, 3)
     fold(1, 4)
+    for ch in range(2):
+        go_lb[4, ch].wait_recv()
+        go_rb[4, ch].wait_recv()
+    outs[:, KA:D] = (
+        outs[:, KA:D].astype(F32)
+        + (
+            comb_b[place_of(0)].astype(F32) + zl_b[3].astype(F32) + zr_b[3].astype(F32)
+        ).reshape(NY * TOK, KB)
+    ).astype(BF)
+    shared_b = shared_far(cols_b)
     fold(0, 4)
-
-    back_p.wait_recv()
-    back_m.wait_recv()
     for copy in sent_kv:
         copy.wait_recv()
     moved[...] = (
         kvs[0].astype(F32) + kvr[0].astype(F32) + kvr[1].astype(F32) + kvr[2].astype(F32)
     ).astype(BF)
-    total = outs[0:TOK, :].astype(F32) + rss[0].astype(F32) + rss[1].astype(F32)
-    total = total + comb[home(0):home(0) + TOK, :].astype(F32)
+    shared_b = shared_back(shared_b, cols_b)
+    for copy in shared_a:
+        copy.wait_recv()
     for ch in range(2):
         go_l[4, ch].wait_recv()
         go_r[4, ch].wait_recv()
-    sums[...] = (total + zl[3].astype(F32) + zr[3].astype(F32)).astype(BF)
+    total = outs[0:TOK, 0:KA].astype(F32) + rss[0, :, 0:KA].astype(F32) + rss[1, :, 0:KA].astype(F32)
+    total = total + comb[home(0):home(0) + TOK, :].astype(F32)
+    sums[:, 0:KA] = (total + zl[3].astype(F32) + zr[3].astype(F32)).astype(BF)
+    for copy in shared_b:
+        copy.wait_recv()
+    sums[:, KA:D] = (
+        outs[0:TOK, KA:D].astype(F32) + rss[0, :, KA:D].astype(F32) + rss[1, :, KA:D].astype(F32)
+    ).astype(BF)
     for copy in started:
         copy.wait_send()
 
@@ -450,18 +599,18 @@
     span = NX * TOK
     scratch = [
         V((NZ * TOK, ROW), BF),
-        V((2, 6, 16, D), BF),
-        V((2, NY * span, D), BF),
-        V((2, NY * span, D), BF),
-        V((2, span, D), BF),
-        V((2, 2, span, D), BF),
-        V((2, 6, 16, D), BF),
-        V((2, 8, 16, D), BF),
+        V((2, 6, 16, KA), BF),
+        V((2, 2 * NY, 64, D), BF),
+        V((2, 2 * NY, 64, D), BF),
+        V((2, span, KA), BF),
+        V((2, 2, span, KA), BF),
+        V((2, 6, 16, KA), BF),
+        V((2, 8, 16, KA), BF),
         V((2, HALF, HALF), BF),
-        V((NZ * TOK, D), BF),
-        V((4, TOK, D), BF),
-        V((4, TOK, D), BF),
-        V((NY * TOK, D), BF),
+        V((NZ * TOK, KA), BF),
+        V((4, TOK, KA), BF),
+        V((4, TOK, KA), BF),
+        V((NY * TOK, D + META), BF),
         V((NY * TOK, D), BF),
         V((2, 16, D), BF),
         V((2, TOK, D), BF),
@@ -469,6 +618,13 @@
         V((2, NY * TOK, SFB), BF),
         V((4, 16, KVW), BF),
         V((3, 16, KVW), BF),
+        V((NZ, NY, TOK, KB + META), BF),
+        V((2, 6, NY, 16, KB), BF),
+        V((2, 8, NY, 16, KB), BF),
+        V((NZ, NY, TOK, KB), BF),
+        V((4, NY, TOK, KB), BF),
+        V((4, NY, TOK, KB), BF),
+        V((2, NY, HALF, HALF), BF),
     ]
     for _ in range(2):
         scratch += [

time: 141 us -> 117 us (0.83)
  Pallas kernels: 139 us -> 115 us
    pallas_call x1, Pallas kernels: 137 us -> 113 us  [shards(): pl.pallas_call(kernel, name='verify_ffn', out_shape=(jax.ShapeDtypeStruct...]
where the time goes in v4:
time: 117 us; the launch traced here: 116 us
  Pallas kernels  115 us (98%)
    pallas_call x1, Pallas kernels, shards(): pl.pallas_call(kernel, name='verify_ffn', out_shape=(jax.ShapeDtypeStruct...  113 us

profile of v4, /device:TPU:2, one launch (start us, length us, event | category | flops | bytes accessed | tf_op | source)
XLA Modules:
  0.0 115.6 jit_solution(15290804293787432453)
XLA Ops:
  0.6 113.4 %verify_ffn.1 = (bf16[32,2560]{1,0:T(8,128)(2,1)}, bf16[16,1024]{1,0:T(8,128)(2,1)}) custom-call(bf16[32,2560]{1,0:T(8,128)(2,1)} %hidden.1, f32[2560]{0:T(1024)} %gain.1, bf16[64,2560]{1,0:T(8,128)(2,1)} %bitcast.9, s32[6,32]{1,0:T(8,128)} %bitcast.10, s32[1,8]{1,0:T(1,128)} %path.1, s32[1,32]{1,0:T(1,128)} %bitcast.11, s32[1,32]{1,0:T(1,128)} %bitcast.12, ...), custom_call_target="tpu_custom_call" | custom-call | tf_op jit(solution)/shard_map/verify_ffn/pallas_call | solution.py:639
  114.0 1.6 %place.1 = (bf16[32,2560]{1,0:T(8,128)(2,1)}, bf16[16,1024]{1,0:T(8,128)(2,1)}) custom-call(bf16[32,2560]{1,0:T(8,128)(2,1)} %get-tuple-element.4.sums, bf16[16,1024]{1,0:T(8,128)(2,1)} %get-tuple-element.5.moved), custom_call_target="tpu_custom_call" | custom-call | tf_op jit(solution)/shard_map/place/pallas_call | solution.py:657
